TPU v7x, 32 devices: a whole 2x2x4 slice. The times are simulated.
32 devices in a mesh: dp: 4 (over z), gx: 4 (over x, core), gy: 2 (over y).
Axes of the slice: x: 2, y: 2, z: 4, core: 2. Of those that a mesh axis runs over, the one named last changes fastest.
Arguments:
- inputs: bfloat16 [4, 1024, 2048], P('dp', None, 'gx'), may hold values from -6 to 6
- lengths: int32 [4], P('dp'), may hold values from 256 to 1024, as said below
- grad_out: bfloat16 [4, 1024, 2048], P('dp', None, 'gx'), may hold values from -6 to 6
- gain_mix: float32 [2048], P('gx'), may hold values from 0.5 to 1.5
- input_weight: bfloat16 [2048, 2816], P('gx', 'gy'), may hold values from -0.125 to 0.125
- branch_weight: bfloat16 [2048, 2816], P('gx', 'gy'), may hold values from -0.125 to 0.125
- conv_w: float32 [4, 2816], P(None, 'gy'), may hold values from -3 to 3
- conv_b: float32 [2816], P('gy'), may hold values from -3 to 3
- gate_a: bfloat16 [16, 176, 176], P('gy'), may hold values from -0.4375 to 0.4375
- bias_a: float32 [2816], P('gy'), may hold values from -4 to 4
- gate_x: bfloat16 [16, 176, 176], P('gy'), may hold values from -0.4375 to 0.4375
- bias_x: float32 [2816], P('gy'), may hold values from -4 to 4
- lam: float32 [2816], P('gy'), may hold values from 2 to 7
- output_weight: bfloat16 [2816, 2048], P('gy', 'gx'), may hold values from -0.3125 to 0.3125
- gain_mlp: float32 [2048], P('gx'), may hold values from 0.5 to 1.5
- gate_weight: bfloat16 [2048, 6144], P('gx', 'gy'), may hold values from -0.125 to 0.125
- up_weight: bfloat16 [2048, 6144], P('gx', 'gy'), may hold values from -0.125 to 0.125
- down_weight: bfloat16 [6144, 2048], P('gy', 'gx'), may hold values from -0.125 to 0.125
Outputs:
- output: bfloat16 [4, 1024, 2048], P('dp', None, 'gx')
- grad_inputs: bfloat16 [4, 1024, 2048], P('dp', None, 'gx')
- grad_gain_mix: float32 [2048], P('gx')
- grad_w_in: float32 [2048, 2816], P('gx', 'gy')
- grad_w_branch: float32 [2048, 2816], P('gx', 'gy')
- grad_conv_w: float32 [4, 2816], P(None, 'gy')
- grad_conv_b: float32 [2816], P('gy')
- grad_gate_a: float32 [16, 176, 176], P('gy')
- grad_bias_a: float32 [2816], P('gy')
- grad_gate_x: float32 [16, 176, 176], P('gy')
- grad_bias_x: float32 [2816], P('gy')
- grad_lam: float32 [2816], P('gy')
- grad_w_out: float32 [2816, 2048], P('gy', 'gx')
- grad_gain_mlp: float32 [2048], P('gx')
- grad_w_g: float32 [2048, 6144], P('gx', 'gy')
- grad_w_u: float32 [2048, 6144], P('gx', 'gy')
- grad_w_d: float32 [6144, 2048], P('gy', 'gx')
- rms_out: float32 [], replicated
- rms_grad: float32 [], replicated
Inputs may be any that keep to these rules, and one draw needn't show every extreme that they name: `lengths`: valid tokens of each sequence, a prefix of its 1024 slots; in every draw one sequence fills all 1024 slots and one has a quarter of them.
All inputs are finite; a program needn't handle non-finite values.
Results may differ from a plain program's by a relative error of at most 0.0095.
Values may be sent and summed in bfloat16 or wider, within the bound.
No kernel may reach another device: no remote copies, remote signals or barrier semaphores. Data moves between devices by JAX's collectives and lax.ppermute only.
A program may use at most 256 MiB of HBM per device.

v0:
```python
import jax
import jax.numpy as jnp
from jax import lax
from jax.sharding import PartitionSpec as P

D = 2048


decay_power = 8.0
norm_eps = 1e-06


def smooth_gate(pre_act):
    return jax.nn.gelu(pre_act, approximate=True)


def gated_product(gate_pre, value_in):
    return smooth_gate(gate_pre) * value_in


def linear_state(decay_rate, drive_term):

    def combine(earlier, later):
        return (earlier[0] * later[0], later[0] * earlier[1] + later[1])

    return lax.associative_scan(combine, (decay_rate, drive_term), axis=1)[1]


def recurrence(gate_pre, input_pre, conv_vals, lam_part):
    log_decay = -decay_power * jax.nn.sigmoid(gate_pre) * jax.nn.softplus(-lam_part)
    decay_rate = jnp.exp(log_decay)
    drive_term = jnp.sqrt(-jnp.expm1(2.0 * log_decay)) * jax.nn.sigmoid(input_pre) * conv_vals
    return linear_state(decay_rate, drive_term)


def causal_conv(inner_projected, conv_part, bias_part):
    taps = conv_part.shape[0]
    length = inner_projected.shape[1]
    padded = jnp.pad(inner_projected, ((0, 0), (taps - 1, 0), (0, 0)))
    conv_total = jnp.zeros_like(inner_projected) + bias_part
    for offset in range(taps):
        conv_total = (
            conv_total
            + conv_part[offset] * padded[:, taps - 1 - offset : taps - 1 - offset + length]
        )
    return conv_total


def row_total(values):
    return lax.psum(values, "gx")


def column_total(values):
    return lax.psum(values, "gy")


def norm_forward(values, gain_vec):
    scale_rows = lax.rsqrt(row_total(jnp.sum(values * values, axis=1)) / D + norm_eps)[:, None]
    unit_rows = values * scale_rows
    return (unit_rows, scale_rows, (unit_rows * gain_vec).astype(jnp.bfloat16))


def norm_backward(grad_normed, unit_rows, scale_rows, gain_vec):
    scaled = grad_normed * gain_vec
    project = row_total(jnp.sum(scaled * unit_rows, axis=1))[:, None] / D
    return (scale_rows * (scaled - unit_rows * project), jnp.sum(grad_normed * unit_rows, axis=0))


def contract_rows(left, right):
    return lax.dot_general(
        left, right, (((0,), (0,)), ((), ())), preferred_element_type=jnp.float32
    )


def times_transpose(left, right):
    return lax.dot_general(
        left, right, (((1,), (1,)), ((), ())), preferred_element_type=jnp.float32
    )


def place_part(part_value, full_shape, offset, axis_dim):
    return lax.dynamic_update_slice_in_dim(
        jnp.zeros(full_shape, jnp.float32), part_value, offset, axis_dim
    )


def body(
    inputs,
    lengths,
    grad_out,
    gain_mix,
    input_weight,
    branch_weight,
    conv_w,
    conv_b,
    gate_a,
    bias_a,
    gate_x,
    bias_x,
    lam,
    output_weight,
    gain_mlp,
    gate_weight,
    up_weight,
    down_weight,
):
    groups = lax.axis_size("gx")
    column = lax.axis_index("gx")
    seq_count, length, local_width = inputs.shape
    row_count = seq_count * length
    mix_part = input_weight.shape[1] // groups
    block_part = gate_a.shape[0] // groups
    block_size = gate_a.shape[1]
    positions = lax.broadcasted_iota(jnp.int32, (seq_count, length), 1)
    valid_rows = (positions < lengths[:, None]).astype(jnp.float32).reshape(row_count, 1)
    channel_start = column * mix_part
    block_start = column * block_part
    conv_part = lax.dynamic_slice_in_dim(conv_w, channel_start, mix_part, 1)
    conv_bias = lax.dynamic_slice_in_dim(conv_b, channel_start, mix_part, 0)
    bias_a_part = lax.dynamic_slice_in_dim(bias_a, channel_start, mix_part, 0)
    bias_x_part = lax.dynamic_slice_in_dim(bias_x, channel_start, mix_part, 0)
    lam_part = lax.dynamic_slice_in_dim(lam, channel_start, mix_part, 0)
    gate_a_part = lax.dynamic_slice_in_dim(gate_a, block_start, block_part, 0)
    gate_x_part = lax.dynamic_slice_in_dim(gate_x, block_start, block_part, 0)
    residual = inputs.astype(jnp.float32).reshape(row_count, local_width)
    unit_mix, scale_mix, normed_mix = norm_forward(residual, gain_mix)
    inner_projected, gating_branch = (
        lax.psum_scatter(
            jnp.dot(normed_mix, input_weight, preferred_element_type=jnp.float32),
            "gx",
            scatter_dimension=1,
            tiled=True,
        ),
        lax.psum_scatter(
            jnp.dot(normed_mix, branch_weight, preferred_element_type=jnp.float32),
            "gx",
            scatter_dimension=1,
            tiled=True,
        ),
    )
    inner_seq = inner_projected.reshape(seq_count, length, mix_part)
    conv_out, conv_pull = jax.vjp(causal_conv, inner_seq, conv_part, conv_bias)
    conv_low = conv_out.astype(jnp.bfloat16)
    conv_blocks = conv_low.reshape(seq_count, length, block_part, block_size)
    gate_pre = (
        jnp.einsum(
            "slnb,nbc->slnc", conv_blocks, gate_a_part, preferred_element_type=jnp.float32
        ).reshape(seq_count, length, mix_part)
        + bias_a_part
    )
    input_pre = (
        jnp.einsum(
            "slnb,nbc->slnc", conv_blocks, gate_x_part, preferred_element_type=jnp.float32
        ).reshape(seq_count, length, mix_part)
        + bias_x_part
    )
    lru_state, state_pull = jax.vjp(
        recurrence, gate_pre, input_pre, conv_low.astype(jnp.float32), lam_part
    )
    mixed_value, mixed_pull = jax.vjp(
        gated_product, gating_branch.reshape(seq_count, length, mix_part), lru_state
    )
    mixer_result = mixed_value.astype(jnp.bfloat16).reshape(row_count, mix_part)
    mixed_full = lax.all_gather(mixer_result, "gx", axis=1, tiled=True)
    middle_residual = residual + column_total(
        jnp.dot(mixed_full, output_weight, preferred_element_type=jnp.float32)
    )
    unit_mlp, scale_mlp, normalized_feedforward = norm_forward(middle_residual, gain_mlp)
    feedforward_gate, feedforward_up = (
        lax.psum_scatter(
            jnp.dot(normalized_feedforward, gate_weight, preferred_element_type=jnp.float32),
            "gx",
            scatter_dimension=1,
            tiled=True,
        ),
        lax.psum_scatter(
            jnp.dot(normalized_feedforward, up_weight, preferred_element_type=jnp.float32),
            "gx",
            scatter_dimension=1,
            tiled=True,
        ),
    )
    hidden_value, hidden_pull = jax.vjp(gated_product, feedforward_gate, feedforward_up)
    hidden_activation = hidden_value.astype(jnp.bfloat16)
    hidden_full = lax.all_gather(hidden_activation, "gx", axis=1, tiled=True)
    final = middle_residual + column_total(
        jnp.dot(hidden_full, down_weight, preferred_element_type=jnp.float32)
    )
    grad_top = grad_out.astype(jnp.float32).reshape(row_count, local_width) * valid_rows
    grad_low = grad_top.astype(jnp.bfloat16)
    grad_w_d = contract_rows(hidden_full, grad_low)
    grad_hidden = lax.psum_scatter(
        times_transpose(grad_low, down_weight), "gx", scatter_dimension=1, tiled=True
    )
    grad_gate_mlp, grad_up_mlp = hidden_pull(grad_hidden)
    gate_grad_full, up_grad_full = (
        lax.all_gather(grad_gate_mlp.astype(jnp.bfloat16), "gx", axis=1, tiled=True),
        lax.all_gather(grad_up_mlp.astype(jnp.bfloat16), "gx", axis=1, tiled=True),
    )
    grad_w_g = contract_rows(normalized_feedforward, gate_grad_full)
    grad_w_u = contract_rows(normalized_feedforward, up_grad_full)
    grad_normed_mlp = column_total(
        times_transpose(gate_grad_full, gate_weight) + times_transpose(up_grad_full, up_weight)
    )
    grad_middle_norm, grad_gain_mlp = norm_backward(grad_normed_mlp, unit_mlp, scale_mlp, gain_mlp)
    grad_middle = grad_top + grad_middle_norm
    grad_mid_low = grad_middle.astype(jnp.bfloat16)
    grad_w_out = contract_rows(mixed_full, grad_mid_low)
    grad_mixed = lax.psum_scatter(
        times_transpose(grad_mid_low, output_weight), "gx", scatter_dimension=1, tiled=True
    ).reshape(seq_count, length, mix_part)
    grad_branch, grad_state = mixed_pull(grad_mixed)
    grad_gate_pre, grad_input_pre, grad_conv_direct, grad_lam_part = state_pull(grad_state)
    gate_low = grad_gate_pre.astype(jnp.bfloat16)
    input_low = grad_input_pre.astype(jnp.bfloat16)
    gate_low_blocks = gate_low.reshape(seq_count, length, block_part, block_size)
    input_low_blocks = input_low.reshape(seq_count, length, block_part, block_size)
    grad_gate_a_part = jnp.einsum(
        "slnb,slnc->nbc", conv_blocks, gate_low_blocks, preferred_element_type=jnp.float32
    )
    grad_gate_x_part = jnp.einsum(
        "slnb,slnc->nbc", conv_blocks, input_low_blocks, preferred_element_type=jnp.float32
    )
    grad_bias_a_part = jnp.sum(gate_low.astype(jnp.float32), axis=(0, 1))
    grad_bias_x_part = jnp.sum(input_low.astype(jnp.float32), axis=(0, 1))
    grad_conv_out = grad_conv_direct + jnp.einsum(
        "slnc,nbc->slnb", gate_low_blocks, gate_a_part, preferred_element_type=jnp.float32
    ).reshape(seq_count, length, mix_part)
    grad_conv_out = grad_conv_out + jnp.einsum(
        "slnc,nbc->slnb", input_low_blocks, gate_x_part, preferred_element_type=jnp.float32
    ).reshape(seq_count, length, mix_part)
    grad_inner, grad_conv_part, grad_conv_bias = conv_pull(grad_conv_out)
    inner_grad_full, branch_grad_full = (
        lax.all_gather(
            grad_inner.astype(jnp.bfloat16).reshape(row_count, mix_part), "gx", axis=1, tiled=True
        ),
        lax.all_gather(
            grad_branch.astype(jnp.bfloat16).reshape(row_count, mix_part), "gx", axis=1, tiled=True
        ),
    )
    grad_w_in = contract_rows(normed_mix, inner_grad_full)
    grad_w_branch = contract_rows(normed_mix, branch_grad_full)
    grad_normed_mix = column_total(
        times_transpose(inner_grad_full, input_weight)
        + times_transpose(branch_grad_full, branch_weight)
    )
    grad_res_norm, grad_gain_mix = norm_backward(grad_normed_mix, unit_mix, scale_mix, gain_mix)
    grad_x = grad_middle + grad_res_norm
    token_here = jnp.where(column == 0, jnp.sum(lengths).astype(jnp.float32), 0.0)
    stat_sums = jnp.stack(
        [jnp.sum(valid_rows * final * final), jnp.sum(valid_rows * grad_x * grad_x), token_here]
    )
    summed_small = lax.psum(
        (
            place_part(grad_conv_part, conv_w.shape, channel_start, 1),
            place_part(grad_conv_bias, conv_b.shape, channel_start, 0),
            place_part(grad_gate_a_part, gate_a.shape, block_start, 0),
            place_part(grad_bias_a_part, bias_a.shape, channel_start, 0),
            place_part(grad_gate_x_part, gate_x.shape, block_start, 0),
            place_part(grad_bias_x_part, bias_x.shape, channel_start, 0),
            place_part(grad_lam_part, lam.shape, channel_start, 0),
            stat_sums,
        ),
        ("dp", "gx"),
    )
    (
        summed_gain_mix,
        summed_w_in,
        summed_w_branch,
        summed_w_out,
        summed_gain_mlp,
        summed_w_g,
        summed_w_u,
        summed_w_d,
    ) = lax.psum(
        (
            grad_gain_mix,
            grad_w_in,
            grad_w_branch,
            grad_w_out,
            grad_gain_mlp,
            grad_w_g,
            grad_w_u,
            grad_w_d,
        ),
        "dp",
    )
    totals = summed_small[7]
    token_count = totals[2] * D
    rms_out = jnp.sqrt(totals[0] / token_count)
    rms_grad = jnp.sqrt(totals[1] / token_count)
    output = final.reshape(seq_count, length, local_width).astype(jnp.bfloat16)
    grad_inputs = grad_x.reshape(seq_count, length, local_width).astype(jnp.bfloat16)
    return (
        output,
        grad_inputs,
        summed_gain_mix,
        summed_w_in,
        summed_w_branch,
        summed_small[0],
        summed_small[1],
        summed_small[2],
        summed_small[3],
        summed_small[4],
        summed_small[5],
        summed_small[6],
        summed_w_out,
        summed_gain_mlp,
        summed_w_g,
        summed_w_u,
        summed_w_d,
        rms_out,
        rms_grad,
    )


def solution(mesh):
    placed = (
        P("dp", None, "gx"),
        P("dp"),
        P("dp", None, "gx"),
        P("gx"),
        P("gx", "gy"),
        P("gx", "gy"),
        P(None, "gy"),
        P("gy"),
        P("gy", None, None),
        P("gy"),
        P("gy", None, None),
        P("gy"),
        P("gy"),
        P("gy", "gx"),
        P("gx"),
        P("gx", "gy"),
        P("gx", "gy"),
        P("gy", "gx"),
    )
    return jax.shard_map(
        body,
        mesh=mesh,
        in_specs=placed,
        out_specs=(
            P("dp", None, "gx"),
            P("dp", None, "gx"),
            P("gx"),
            P("gx", "gy"),
            P("gx", "gy"),
            P(None, "gy"),
            P("gy"),
            P("gy", None, None),
            P("gy"),
            P("gy", None, None),
            P("gy"),
            P("gy"),
            P("gy", "gx"),
            P("gx"),
            P("gx", "gy"),
            P("gx", "gy"),
            P("gy", "gx"),
            P(),
            P(),
        ),
        check_vma=False,
    )
```

profile of v0, /device:TPU:0, one launch (start us, length us, event | category | flops | bytes accessed | tf_op | source)
XLA Modules:
  0.0 3161.9 jit_solution(8729740351128325871)
XLA Ops:
  35.1 43.7 %reduce-scatter.9.cloned.1.call-done = f32[1024,352]{0,1:T(8,128)} async-done(((f32[1024,1408]{0,1:T(8,128)}), f32[1024,352]{0,1:T(8,128)}) %reduce-scatter.9.cloned.1.call-update) | async-done | bytes 1441808 | tf_op jit(solution)/shard_map/reduce_scatter | solution.py:128
  87.3 28.5 slice.347
  115.9 28.3 slice.352
  144.2 28.3 slice.348
  177.8 28.7 slice.420
  206.5 28.3 slice.350
  234.8 28.3 slice.349
  299.6 17.0 slice.356
  639.5 28.6 pad.422
  668.1 28.9 pad.423
  701.4 27.2 all-gather.16.cloned.1.call-done
  742.7 54.3 %all-reduce.115.cloned.1.call-done = f32[1024,512]{1,0:T(8,128)} async-done(((f32[1024,512]{1,0:T(8,128)}), f32[1024,512]{1,0:T(8,128)}) %all-reduce.115.cloned.1.call-update) | async-done | bytes 2097168 | tf_op jit(solution)/shard_map/psum | solution.py:54
  830.6 68.1 %reduce-scatter.15.cloned.1.call-done = f32[1024,768]{1,0:T(8,128)} async-done(((f32[1024,3072]{1,0:T(8,128)}), f32[1024,768]{1,0:T(8,128)}) %reduce-scatter.15.cloned.1.call-update) | async-done | bytes 3145744 | tf_op jit(solution)/shard_map/reduce_scatter | solution.py:192
  898.7 101.7 %reduce-scatter.11.cloned.1.call-done = f32[1024,768]{1,0:T(8,128)} async-done(((f32[1024,3072]{1,0:T(8,128)}), f32[1024,768]{1,0:T(8,128)}) %reduce-scatter.11.cloned.1.call-update) | async-done | bytes 3145744 | tf_op jit(solution)/shard_map/reduce_scatter | solution.py:170
  1000.4 101.8 %reduce-scatter.13.cloned.1.call-done = f32[1024,768]{1,0:T(8,128)} async-done(((f32[1024,3072]{1,0:T(8,128)}), f32[1024,768]{1,0:T(8,128)}) %reduce-scatter.13.cloned.1.call-update) | async-done | bytes 3145744 | tf_op jit(solution)/shard_map/reduce_scatter | solution.py:176
  1110.8 45.0 %all-gather.10.cloned.1.call-done = bf16[1024,3072]{1,0:T(8,128)(2,1)} async-done(((bf16[1024,768]{1,0:T(8,128)(2,1)}), bf16[1024,3072]{1,0:T(8,128)(2,1)}) %all-gather.10.cloned.1.call-update) | async-done | bytes 6291472 | tf_op jit(solution)/shard_map/all_gather | solution.py:185
  1163.3 41.1 %all-gather.12.cloned.1.call-done = bf16[1024,3072]{1,0:T(8,128)(2,1)} async-done(((bf16[1024,768]{1,0:T(8,128)(2,1)}), bf16[1024,3072]{1,0:T(8,128)(2,1)}) %all-gather.12.cloned.1.call-update) | async-done | bytes 6291472 | tf_op jit(solution)/shard_map/all_gather | solution.py:197
  1212.9 40.0 %all-gather.14.cloned.1.call-done = bf16[1024,3072]{1,0:T(8,128)(2,1)} async-done(((bf16[1024,768]{1,0:T(8,128)(2,1)}), bf16[1024,3072]{1,0:T(8,128)(2,1)}) %all-gather.14.cloned.1.call-update) | async-done | bytes 6291472 | tf_op jit(solution)/shard_map/all_gather | solution.py:198
  1260.7 108.3 %all-reduce.123.cloned.1.call-done = (f32[1024,512]{1,0:T(8,128)}, f32[1024,512]{1,0:T(8,128)}) async-done(((f32[1024,512]{1,0:T(8,128)}, f32[1024,512]{1,0:T(8,128)}), (f32[1024,512]{1,0:T(8,128)}, f32[1024,512]{1,0:T(8,128)})) %all-reduce.123.cloned.1.call-update) | async-done | bytes 4194320 | tf_op jit(solution)/shard_map/psum | solution.py:54
  1388.5 54.1 %reduce-scatter.17.cloned.1.call-done = f32[1024,352]{0,1:T(8,128)} async-done(((f32[1024,1408]{0,1:T(8,128)}), f32[1024,352]{0,1:T(8,128)}) %reduce-scatter.17.cloned.1.call-update) | async-done | bytes 1441808 | tf_op jit(solution)/shard_map/reduce_scatter | solution.py:209
  1450.3 28.5 slice.422
  1478.8 27.8 slice.421
  1823.2 26.9 pad.489
  1853.4 28.8 pad.518
  1882.2 27.1 pad.491
  1909.3 26.9 pad.517
  1936.1 27.0 pad.490
  1963.2 27.0 pad.426
  2077.8 24.2 all-reduce.117.cloned.1.call-done
  2116.4 61.1 %all-reduce.104 = (f32[4,1408]{1,0:T(4,128)}, f32[1408]{0:T(1024)}, f32[1408]{0:T(1024)}, f32[1408]{0:T(1024)}, f32[1408]{0:T(1024)}, /*index=5*/f32[3]{0:T(128)S(1)}) all-reduce(f32[4,1408]{1,0:T(4,128)S(1)} %dynamic_update_slice.21, f32[1408]{0:T(1024)S(1)} %dynamic_update_slice.22, ...), channel_id=1, replica_groups=mesh['dp'=4,'gx'=4,'gy'=2] {'dp','gx'}, use_global_device_ids=true, to_apply=%region_26.27 | all-reduce | flops 11267 | bytes 90136 | tf_op jit(solution)/shard_map/psum | solution.py:253
  2189.2 20.0 all-reduce.119.cloned.1.call-done
  2209.2 919.7 %all-reduce.121.cloned.1.call-done = (f32[512,1408]{1,0:T(8,128)}, f32[512,1408]{1,0:T(8,128)}, f32[1408,512]{1,0:T(8,128)}, f32[512,3072]{1,0:T(8,128)}, f32[512,3072]{1,0:T(8,128)}, /*index=5*/f32[3072,512]{1,0:T(8,128)}) async-done(((f32[512,1408]{1,0:T(8,128)}, f32[512,1408]{1,0:T(8,128)}, f32[1408,512]{1,0:T(8,128)}, f32[512,3072]{1,0:T(8,128)}, f32[512,3072]{1,0:T(8,128)}, ...) | async-done | bytes 27525136 | tf_op jit(solution)/shard_map/psum | solution.py:275
  (659 shorter events, 965.3 us)
Async XLA Ops:
  7.2 727.5 %copy-start = (bf16[3072,512]{1,0:T(8,128)(2,1)S(1)}, bf16[3072,512]{1,0:T(8,128)(2,1)}, u32[]{:S(2)}) copy-start(bf16[3072,512]{1,0:T(8,128)(2,1)} %param.35) | copy-start | bytes 9437188
  7.2 71.6 %reduce-scatter.9.cloned.1.call-start = ((), (), s32[]{:S(2)}) async-start(), calls=%async_computation.7 | async-start | bytes 7208960 | tf_op jit(solution)/shard_map/reduce_scatter | solution.py:128
  23.3 673.7 %reduce-scatter.7.cloned.1.call-start = ((), (), s32[]{:S(2)}) async-start(), calls=%async_computation.6 | async-start | bytes 7208960 | tf_op jit(solution)/shard_map/reduce_scatter | solution.py:134
  30.4 698.2 %all-gather.16.cloned.1.call-start = ((), (), s32[]{:S(2)}) async-start(), calls=%async_computation.17 | async-start | bytes 3604480 | tf_op jit(solution)/shard_map/all_gather | solution.py:164
  33.7 50.0 %copy-start.132 = (f32[352]{0:T(512)}, f32[352]{0:T(512)S(1)}, u32[]{:S(2)}) copy-start(f32[352]{0:T(512)S(1)} %get-tuple-element.34) | copy-start | bytes 4228
  33.7 50.0 %copy-start.134 = (f32[352]{0:T(512)}, f32[352]{0:T(512)S(1)}, u32[]{:S(2)}) copy-start(f32[352]{0:T(512)S(1)} %get-tuple-element.35) | copy-start | bytes 4228
  701.3 95.7 %all-reduce.115.cloned.1.call-start = ((), (), s32[]{:S(2)}) async-start(), calls=%async_computation.8 | async-start | bytes 4194304 | tf_op jit(solution)/shard_map/psum | solution.py:54
  734.0 164.8 %reduce-scatter.15.cloned.1.call-start = ((), (), s32[]{:S(2)}) async-start(), calls=%async_computation.12 | async-start | bytes 15728640 | tf_op jit(solution)/shard_map/reduce_scatter | solution.py:192
  742.5 64.8 %copy-start.137 = (f32[512]{0:T(512)S(1)}, f32[512]{0:T(512)}, u32[]{:S(2)}) copy-start(f32[512]{0:T(512)} %param.32) | copy-start | bytes 6148
  742.5 257.9 %reduce-scatter.11.cloned.1.call-start = ((), (), s32[]{:S(2)}) async-start(), calls=%async_computation.9 | async-start | bytes 15728640 | tf_op jit(solution)/shard_map/reduce_scatter | solution.py:170
  819.4 282.8 %reduce-scatter.13.cloned.1.call-start = ((), (), s32[]{:S(2)}) async-start(), calls=%async_computation.10 | async-start | bytes 15728640 | tf_op jit(solution)/shard_map/reduce_scatter | solution.py:176
  830.5 325.2 %all-gather.10.cloned.1.call-start = ((), (), s32[]{:S(2)}) async-start(), calls=%async_computation.11 | async-start | bytes 7864320 | tf_op jit(solution)/shard_map/all_gather | solution.py:185
  1109.2 95.2 %all-gather.12.cloned.1.call-start = ((), (), s32[]{:S(2)}) async-start(), calls=%async_computation.13 | async-start | bytes 7864320 | tf_op jit(solution)/shard_map/all_gather | solution.py:197
  1109.9 142.9 %all-gather.14.cloned.1.call-start = ((), (), s32[]{:S(2)}) async-start(), calls=%async_computation.14 | async-start | bytes 7864320 | tf_op jit(solution)/shard_map/all_gather | solution.py:198
  1110.5 258.5 %all-reduce.123.cloned.1.call-start = ((), (), s32[]{:S(2)}) async-start(), calls=%async_computation.22 | async-start | bytes 8388608 | tf_op jit(solution)/shard_map/psum | solution.py:54
  1163.3 89.6 %copy-start.142 = (bf16[512,3072]{1,0:T(8,128)(2,1)S(1)}, bf16[512,3072]{1,0:T(8,128)(2,1)}, u32[]{:S(2)}) copy-start(bf16[512,3072]{1,0:T(8,128)(2,1)} %param.34) | copy-start | bytes 9437188
  1260.6 108.4 %copy-start.9 = (f32[1024,512]{1,0:T(8,128)S(1)}, f32[1024,512]{1,0:T(8,128)}, u32[]{:S(2)}) copy-start(f32[1024,512]{1,0:T(8,128)} %get-tuple-element.80) | copy-start | bytes 6291460
  1260.7 181.9 %reduce-scatter.17.cloned.1.call-start = ((), (), s32[]{:S(2)}) async-start(), calls=%async_computation.15 | async-start | bytes 7208960 | tf_op jit(solution)/shard_map/reduce_scatter | solution.py:209
  1388.4 54.1 %copy-start.14 = (f32[1024,352]{0,1:T(8,128)S(1)}, f32[1024,352]{0,1:T(8,128)}, u32[]{:S(2)}) copy-start(f32[1024,352]{0,1:T(8,128)} %reduce-scatter.7.cloned.1.call-done) | copy-start | bytes 4325380
  1388.4 54.1 %copy-start.38 = (f32[1,1024,352]{1,2,0:T(8,128)S(1)}, f32[1,1024,352]{1,2,0:T(8,128)}, u32[]{:S(2)}) copy-start(f32[1,1024,352]{1,2,0:T(8,128)} %get-tuple-element.82) | copy-start | bytes 4325380
  1388.5 625.6 %all-gather.20.cloned.1.call-start = ((), (), s32[]{:S(2)}) async-start(), calls=%async_computation.19 | async-start | bytes 3604480 | tf_op jit(solution)/shard_map/all_gather | solution.py:237
  1445.9 587.0 %all-gather.18.cloned.1.call-start = ((), (), s32[]{:S(2)}) async-start(), calls=%async_computation.18 | async-start | bytes 3604480 | tf_op jit(solution)/shard_map/all_gather | solution.py:234
  1450.3 56.3 %copy-start.17 = (f32[1,512,352]{1,2,0:T(8,128)S(1)}, f32[1,512,352]{1,2,0:T(8,128)}, u32[]{:S(2)}) copy-start(f32[1,512,352]{1,2,0:T(8,128)} %pad.421) | copy-start | bytes 2162692
  1450.3 56.3 %copy-start.19 = (f32[1,512,352]{1,2,0:T(8,128)S(1)}, f32[1,512,352]{1,2,0:T(8,128)}, u32[]{:S(2)}) copy-start(f32[1,512,352]{1,2,0:T(8,128)} %pad.420) | copy-start | bytes 2162692
  1450.3 56.3 %copy-start.24 = (f32[1,511,352]{1,2,0:T(8,128)S(1)}, f32[1,511,352]{1,2,0:T(8,128)}, u32[]{:S(2)}) copy-start(f32[1,511,352]{1,2,0:T(8,128)} %slice.347) | copy-start | bytes 2158468
  1506.6 234.8 %copy-start.46 = (f32[1,512,352]{1,2,0:T(8,128)}, f32[1,512,352]{1,2,0:T(8,128)S(1)}, u32[]{:S(2)}) copy-start(f32[1,512,352]{1,2,0:T(8,128)S(1)} %slice.421) | copy-start | bytes 2162692
  1541.9 199.5 %copy-start.85 = (f32[1,256,352]{1,2,0:T(8,128)}, f32[1,256,352]{1,2,0:T(8,128)S(1)}, u32[]{:S(2)}) copy-start(f32[1,256,352]{1,2,0:T(8,128)S(1)} %slice.423) | copy-start | bytes 1081348
  1936.1 54.1 %slice-start.7 = ((f32[1,512,352]{1,2,0:T(8,128)}), f32[1,1,352]{1,2,0:T(8,128)S(1)}, s32[]{:S(2)}) async-start(f32[1,512,352]{1,2,0:T(8,128)} %copy-done.46), calls=%async_computation.30 | async-start | bytes 360448 | tf_op jit(solution)/shard_map/transpose(jvp())/split | solution.py:26
  1994.7 63.8 %copy-start.20 = (bf16[1,1024,352]{1,2,0:T(8,128)(2,1)}, bf16[1,1024,352]{1,2,0:T(8,128)(2,1)S(1)}, u32[]{:S(2)}) copy-start(bf16[1,1024,352]{1,2,0:T(8,128)(2,1)S(1)} %get-tuple-element.59) | copy-start | bytes 2162692
  2005.6 96.4 %all-reduce.117.cloned.1.call-start = ((), (), s32[]{:S(2)}) async-start(), calls=%async_computation.16 | async-start | bytes 4194304 | tf_op jit(solution)/shard_map/psum | solution.py:54
  2038.9 170.3 %all-reduce.119.cloned.1.call-start = ((), (), s32[]{:S(2)}) async-start(), calls=%async_computation.20 | async-start | bytes 5767168 | tf_op jit(solution)/shard_map/psum | solution.py:253
  2060.1 1068.9 %all-reduce.121.cloned.1.call-start = ((), (), s32[]{:S(2)}) async-start(), calls=%async_computation.21 | async-start | bytes 55050240 | tf_op jit(solution)/shard_map/psum | solution.py:275
  (139 other events, 1289.5 us)
Sparse Core Ops, SparseCore 0:
  23.4 55.2 reduce-scatter.8
  82.1 54.8 reduce-scatter.6
  701.4 27.0 all-gather.15
  734.1 62.9 all-reduce.114
  799.6 99.0 reduce-scatter.14
  901.3 99.0 reduce-scatter.10
  1003.2 99.0 reduce-scatter.12
  1109.3 46.3 all-gather.9
  1158.0 46.3 all-gather.11
  1206.4 46.3 all-gather.13
  1260.8 108.2 all-reduce.122
  1388.6 53.9 reduce-scatter.16
  1446.0 27.0 all-gather.19
  2005.7 27.0 all-gather.17
  2039.0 62.9 all-reduce.116
  2106.7 102.4 all-reduce.118
  2214.1 914.8 all-reduce.120
where the time goes:
time: 3170 us; the launch traced here: 3160 us
  waiting for transfers between devices  1660 us (52%)
  local copies, waits for them, and re-layouts  1090 us (34%)
  other arithmetic  158 us (5%)
  matrix products  129 us (4%)
  blocking collectives  99.1 us (3%)
    psum x1, waiting for transfers between devices, body(): lax.psum((grad_gain_mix, grad_w_in, grad_w_branch, grad_w_out, grad_gain_...  920 us
    pad x79, local copies, waits for them, and re-layouts, linear_state(): return lax.associative_scan(combine, (decay_rate, drive_term), axis=1)[1]  524 us
    slice x74, local copies, waits for them, and re-layouts, linear_state(): return lax.associative_scan(combine, (decay_rate, drive_term), axis=1)[1]  514 us
    psum x3, waiting for transfers between devices, column_total(): return lax.psum(values, 'gy')  187 us
    reduce_scatter x1, waiting for transfers between devices, body(): lax.psum_scatter(jnp.dot(normalized_feedforward, up_weight, preferred_ele...  102 us
    reduce_scatter x1, waiting for transfers between devices, body(): lax.psum_scatter(jnp.dot(normalized_feedforward, gate_weight, preferred_e...  102 us
    reduce_scatter x1, waiting for transfers between devices, body(): lax.psum_scatter(times_transpose(grad_low, down_weight), 'gx', scatter_di...  68.1 us
  transfers between devices with their start and end apart: 17, of which 15 were waited for; matrix products, arithmetic and copies ran while one was open for 41% of the time, Pallas kernels for 0%

commit v1 on v0

v1 whole, which is shorter than its diff:
```python
import jax
import jax.numpy as jnp
from jax import lax
from jax.experimental import pallas as pl
from jax.experimental.pallas import tpu as pltpu
from jax.sharding import PartitionSpec as P

bf16 = jnp.bfloat16
f32 = jnp.float32
SQRT_2_OVER_PI = 0.7978845608028654
CHUNKS = 8
STEP = 32


def expm1_neg(y):
    series = 1.0 + y * (1.0 / 9.0)
    for order in range(8, 1, -1):
        series = 1.0 + y * (1.0 / order) * series
    return jnp.where(y > -0.5, y * series, jnp.exp(y) - 1.0)


def gelu_parts(v):
    tanh_value = jnp.tanh(SQRT_2_OVER_PI * (v + 0.044715 * (v * v * v)))
    half = 0.5 * (1.0 + tanh_value)
    slope = half + 0.5 * v * (1.0 - tanh_value * tanh_value) * (
        SQRT_2_OVER_PI * (1.0 + 3.0 * 0.044715 * (v * v))
    )
    return v * half, slope


def gelu_value(v):
    return 0.5 * v * (1.0 + jnp.tanh(SQRT_2_OVER_PI * (v + 0.044715 * (v * v * v))))


LANES = 128


def slab_put(slabs, rows, values):
    width = values.shape[1]
    for j in range(slabs.shape[0]):
        size = min(LANES, width - j * LANES)
        slabs[j, rows, pl.ds(0, size)] = values[:, j * LANES : j * LANES + size]


def slab_get(slabs, rows, width):
    parts = []
    for j in range(slabs.shape[0]):
        parts.append(slabs[j, rows, pl.ds(0, min(LANES, width - j * LANES))])
    return jnp.concatenate(parts, axis=1)


def chunk_scan(order, rates, rate_shift, values, prefix, carries, width):
    slabs = range(values.shape[0])
    span = prefix.shape[1] // CHUNKS

    def advance(n, carry):
        hidden, product = carry
        s = n if order > 0 else span - 1 - n
        rows = pl.ds(s, CHUNKS, stride=span)
        rate_rows = pl.ds(s + rate_shift, CHUNKS, stride=span)
        next_hidden, next_product = [], []
        for j in slabs:
            rate = rates[j, rate_rows, :]
            next_hidden.append(rate * hidden[j] + values[j, rows, :])
            next_product.append(product[j] * rate)
            values[j, rows, :] = next_hidden[j]
            prefix[j, rows, :] = next_product[j]
        return tuple(next_hidden), tuple(next_product)

    zeros = tuple(jnp.zeros((CHUNKS, LANES), f32) for _ in slabs)
    ones = tuple(jnp.ones((CHUNKS, LANES), f32) for _ in slabs)
    hidden, product = lax.fori_loop(0, span, advance, (zeros, ones), unroll=8)
    for j in slabs:
        size = min(LANES, width - j * LANES)
        entering = jnp.zeros((1, LANES), f32)
        for c in range(CHUNKS) if order > 0 else range(CHUNKS - 1, -1, -1):
            carries[pl.ds(c, 1), pl.ds(j * LANES, size)] = entering[:, :size]
            entering = product[j][c : c + 1] * entering + hidden[j][c : c + 1]


def mixer_forward_kernel(
    joint_ref, tap_ref, conv_bias_ref, gate_a_ref, bias_a_ref, gate_x_ref, bias_x_ref, coef_ref,
    mixed_ref, conv_low_ref, sig_a_ref, sig_x_ref, decay_ref, root_ref, state_ref,
    inner_pad, rates, drive, prefix, carries,
):
    length, width = conv_low_ref.shape
    pitch = joint_ref.shape[1] // 2
    taps = tap_ref.shape[0]
    span = length // CHUNKS
    inner_pad[pl.ds(0, 8), :] = jnp.zeros((8, width), f32)
    inner_pad[pl.ds(8, length), :] = joint_ref[:, pl.ds(0, width)]

    def convolve(i, carry):
        start = pl.multiple_of(i * STEP, STEP)
        total = jnp.broadcast_to(conv_bias_ref[...], (STEP, width))
        window = inner_pad[pl.ds(start, STEP + 8), :]
        for k in range(taps):
            total = total + tap_ref[pl.ds(k, 1), :] * window[8 - k : 8 - k + STEP]
        conv_low_ref[pl.ds(start, STEP), :] = total.astype(bf16)
        return carry

    lax.fori_loop(0, length // STEP, convolve, 0)
    sig_a_ref[...] = jnp.dot(conv_low_ref[...], gate_a_ref[...], preferred_element_type=f32)
    sig_x_ref[...] = jnp.dot(conv_low_ref[...], gate_x_ref[...], preferred_element_type=f32)

    def gates(i, carry):
        rows = pl.ds(pl.multiple_of(i * STEP, STEP), STEP)
        sig_a = jax.nn.sigmoid(sig_a_ref[rows, :] + bias_a_ref[...])
        sig_x = jax.nn.sigmoid(sig_x_ref[rows, :] + bias_x_ref[...])
        log_decay = sig_a * coef_ref[...]
        root = jnp.sqrt(-expm1_neg(2.0 * log_decay))
        sig_a_ref[rows, :] = sig_a
        sig_x_ref[rows, :] = sig_x
        decay = jnp.exp(log_decay)
        decay_ref[rows, :] = decay
        slab_put(rates, rows, decay)
        root_ref[rows, :] = root
        slab_put(drive, rows, root * sig_x * conv_low_ref[rows, :].astype(f32))
        return carry

    lax.fori_loop(0, length // STEP, gates, 0)

    chunk_scan(1, rates, 0, drive, prefix, carries, width)

    def finish(i, carry):
        start = pl.multiple_of(i * STEP, STEP)
        rows = pl.ds(start, STEP)
        state = slab_get(drive, rows, width) + slab_get(prefix, rows, width) * carries[pl.ds(start // span, 1), :]
        state_ref[rows, :] = state
        mixed_ref[rows, :] = (gelu_value(joint_ref[rows, pl.ds(pitch, width)]) * state).astype(bf16)
        return carry

    lax.fori_loop(0, length // STEP, finish, 0)


def mixer_forward(joint, taps, conv_bias, gate_a, bias_a, gate_x, bias_x, coef):
    length, width = joint.shape[0], taps.shape[1]
    full = jax.ShapeDtypeStruct((length, width), f32)
    low = jax.ShapeDtypeStruct((length, width), bf16)
    slabs = pl.cdiv(width, LANES)
    return pl.pallas_call(
        mixer_forward_kernel,
        out_shape=(low, low, full, full, full, full, full),
        scratch_shapes=[
            pltpu.VMEM((length + 8, width), f32),
            pltpu.VMEM((slabs, length, LANES), f32),
            pltpu.VMEM((slabs, length, LANES), f32),
            pltpu.VMEM((slabs, length, LANES), f32),
            pltpu.VMEM((CHUNKS, width), f32),
        ],
        cost_estimate=pl.CostEstimate(
            flops=4 * length * width * width, bytes_accessed=32 * length * width, transcendentals=6 * length * width
        ),
        compiler_params=pltpu.CompilerParams(vmem_limit_bytes=48 * 1024 * 1024),
        name="mixer_forward",
    )(joint, taps, conv_bias, gate_a, bias_a, gate_x, bias_x, coef)


def mixer_backward_kernel(
    grad_mixed_ref, joint_ref, conv_low_ref, sig_a_ref, sig_x_ref, decay_ref, root_ref, state_ref,
    tap_ref, gate_a_ref, gate_x_ref, coef_ref, slope_ref,
    grad_joint_ref, gate_low_ref, input_low_ref, small_ref,
    inner_pad, state_pad, rates, gain, prefix, grad_conv, carries,
):
    length, width = conv_low_ref.shape
    pitch = joint_ref.shape[1] // 2
    taps = tap_ref.shape[0]
    span = length // CHUNKS
    steps = length // STEP
    zeros8 = jnp.zeros((8, width), f32)
    inner_pad[pl.ds(0, 8), :] = zeros8
    inner_pad[pl.ds(8, length), :] = joint_ref[:, pl.ds(0, width)]
    grad_joint_ref[...] = jnp.zeros(grad_joint_ref.shape, bf16)
    state_pad[pl.ds(0, 8), :] = zeros8
    slab_put(rates, pl.ds(length, 8), zeros8)
    grad_conv[pl.ds(length, 8), :] = zeros8

    def open_gate(i, carry):
        start = pl.multiple_of(i * STEP, STEP)
        rows = pl.ds(start, STEP)
        value, slope = gelu_parts(joint_ref[rows, pl.ds(pitch, width)])
        grad_mixed = grad_mixed_ref[rows, :]
        state = state_ref[rows, :]
        state_pad[pl.ds(start + 8, STEP), :] = state
        slab_put(rates, rows, decay_ref[rows, :])
        slab_put(gain, rows, grad_mixed * value)
        grad_joint_ref[rows, pl.ds(pitch, width)] = (grad_mixed * state * slope).astype(bf16)
        return carry

    lax.fori_loop(0, steps, open_gate, 0)

    chunk_scan(-1, rates, 1, gain, prefix, carries, width)

    def fold(values):
        return jnp.sum(values.reshape(STEP // 8, 8, width), axis=0)

    def gates(i, sums):
        start = pl.multiple_of(i * STEP, STEP)
        rows = pl.ds(start, STEP)
        q = slab_get(gain, rows, width) + slab_get(prefix, rows, width) * carries[pl.ds(start // span, 1), :]
        sig_a = sig_a_ref[rows, :]
        sig_x = sig_x_ref[rows, :]
        decay = decay_ref[rows, :]
        root = root_ref[rows, :]
        conv = conv_low_ref[rows, :].astype(f32)
        earlier = state_pad[pl.ds(start, STEP + 8), :][7 : 7 + STEP]
        g = q * (earlier * decay - sig_x * conv * (decay * decay) / root)
        rate = q * root
        gate_low = (g * coef_ref[...] * (sig_a * (1.0 - sig_a))).astype(bf16)
        input_low = (rate * conv * (sig_x * (1.0 - sig_x))).astype(bf16)
        gate_low_ref[rows, :] = gate_low
        input_low_ref[rows, :] = input_low
        grad_conv[rows, :] = rate * sig_x
        sum_a, sum_x, sum_lam = sums
        return (
            sum_a + fold(gate_low.astype(f32)),
            sum_x + fold(input_low.astype(f32)),
            sum_lam + fold(sig_a * g),
        )

    sum_a, sum_x, sum_lam = lax.fori_loop(0, steps, gates, (zeros8, zeros8, zeros8))
    contract = (((1,), (1,)), ((), ()))
    grad_conv[pl.ds(0, length), :] += lax.dot_general(
        gate_low_ref[...], gate_a_ref[...], contract, preferred_element_type=f32
    )
    grad_conv[pl.ds(0, length), :] += lax.dot_general(
        input_low_ref[...], gate_x_ref[...], contract, preferred_element_type=f32
    )

    def convolve(i, sums):
        start = pl.multiple_of(i * STEP, STEP)
        ahead = grad_conv[pl.ds(start, STEP + 8), :]
        behind = inner_pad[pl.ds(start, STEP + 8), :]
        here = ahead[:STEP]
        total = jnp.zeros((STEP, width), f32)
        out = []
        for k in range(taps):
            total = total + tap_ref[pl.ds(k, 1), :] * ahead[k : k + STEP]
            out.append(sums[k] + fold(here * behind[8 - k : 8 - k + STEP]))
        out.append(sums[taps] + fold(here))
        grad_joint_ref[pl.ds(start, STEP), pl.ds(0, width)] = total.astype(bf16)
        return tuple(out)

    sums = lax.fori_loop(0, steps, convolve, (zeros8,) * (taps + 1))
    for k in range(taps + 1):
        small_ref[pl.ds(k, 1), :] = jnp.sum(sums[k], axis=0, keepdims=True)
    small_ref[pl.ds(taps + 1, 1), :] = jnp.sum(sum_a, axis=0, keepdims=True)
    small_ref[pl.ds(taps + 2, 1), :] = jnp.sum(sum_x, axis=0, keepdims=True)
    small_ref[pl.ds(taps + 3, 1), :] = jnp.sum(sum_lam, axis=0, keepdims=True) * slope_ref[...]


def mixer_backward(
    grad_mixed, joint, conv_low, sig_a, sig_x, decay, root, state, taps, gate_a, gate_x, coef, slope
):
    length, width = conv_low.shape
    low = jax.ShapeDtypeStruct((length, width), bf16)
    slabs = pl.cdiv(width, LANES)
    return pl.pallas_call(
        mixer_backward_kernel,
        out_shape=(jax.ShapeDtypeStruct(joint.shape, bf16), low, low, jax.ShapeDtypeStruct((taps.shape[0] + 4, width), f32)),
        scratch_shapes=[pltpu.VMEM((length + 8, width), f32)] * 2
        + [pltpu.VMEM((slabs, length + 8, LANES), f32)]
        + [pltpu.VMEM((slabs, length, LANES), f32)] * 2
        + [pltpu.VMEM((length + 8, width), f32), pltpu.VMEM((CHUNKS, width), f32)],
        cost_estimate=pl.CostEstimate(
            flops=4 * length * width * width, bytes_accessed=40 * length * width, transcendentals=2 * length * width
        ),
        compiler_params=pltpu.CompilerParams(vmem_limit_bytes=56 * 1024 * 1024),
        name="mixer_backward",
    )(grad_mixed, joint, conv_low, sig_a, sig_x, decay, root, state, taps, gate_a, gate_x, coef, slope)


norm_eps = 1e-06
decay_power = 8.0


def exchange(value, flip, across=False):
    wide, high = lax.axis_size("gx"), lax.axis_size("gy")
    if not across:
        return lax.ppermute(value, "gx", [(i, i ^ flip) for i in range(wide)])
    if flip == 0:
        return lax.ppermute(value, "gy", [(j, j ^ 1) for j in range(high)])
    return lax.ppermute(
        value,
        ("gx", "gy"),
        [(i * high + j, (i ^ flip) * high + (j ^ 1)) for i in range(wide) for j in range(high)],
    )


def line_gather(value, place, buffer):
    count = lax.axis_size("dp")
    here = lax.axis_index("dp")
    rightward, leftward = [value], [value]
    for _ in range(count - 1):
        rightward.append(lax.ppermute(rightward[-1], "dp", [(i, i + 1) for i in range(count - 1)]))
        leftward.append(lax.ppermute(leftward[-1], "dp", [(i + 1, i) for i in range(count - 1)]))
    buffer = place(buffer, value, here)
    for s in range(1, count):
        arrived = jnp.where(here >= s, rightward[s], leftward[count - s])
        buffer = place(buffer, arrived, jnp.where(here >= s, here - s, here - s + count))
    return buffer


def line_sum(value):
    count = lax.axis_size("dp")
    here = lax.axis_index("dp")
    kind = value.dtype
    if count == 1:
        return value
    half = count // 2
    for s in range(half - 1):
        arrived = lax.ppermute(value, "dp", [(s, s + 1), (count - 1 - s, count - 2 - s)])
        value = (value.astype(f32) + arrived.astype(f32)).astype(kind)
    arrived = lax.ppermute(value, "dp", [(half - 1, half), (half, half - 1)])
    value = (value.astype(f32) + arrived.astype(f32)).astype(kind)
    for s in range(half - 1):
        arrived = lax.ppermute(value, "dp", [(half - 1 - s, half - 2 - s), (half + s, half + s + 1)])
        takes = jnp.logical_or(here == half - 2 - s, here == half + s + 1)
        value = jnp.where(takes, arrived, value)
    return value


def in_order(pieces):
    place = lax.axis_index("gx")
    count = len(pieces)
    bit = 1
    while bit < count:
        swapped = jnp.bitwise_and(place, bit) != 0
        pieces = [jnp.where(swapped, pieces[r ^ bit], pieces[r]) for r in range(count)]
        bit *= 2
    return pieces


def halves(mine, other):
    side = lax.axis_index("gy")
    return jnp.where(
        side == 0, jnp.concatenate([mine, other], axis=0), jnp.concatenate([other, mine], axis=0)
    )


def my_half(values, other=False):
    rows = values.shape[0] // lax.axis_size("gy")
    side = lax.axis_index("gy")
    return lax.dynamic_slice_in_dim(values, ((1 - side) if other else side) * rows, rows, 0)


def plane_scatter(pieces):
    low = [p.astype(bf16) for p in pieces]
    kept = pieces[0] + exchange(low[1], 1).astype(f32)
    passed = (pieces[2] + exchange(low[3], 1).astype(f32)).astype(bf16)
    side = exchange(my_half(kept, other=True).astype(bf16), 0, across=True)
    along = exchange(my_half(passed), 2)
    corner = exchange(my_half(passed, other=True), 2, across=True)
    return (my_half(kept) + side.astype(f32)) + (along.astype(f32) + corner.astype(f32))


def plane_gather(block):
    along, side, corner = exchange(block, 2), exchange(block, 0, across=True), exchange(block, 2, across=True)
    mate, mate_along = exchange(block, 1), exchange(along, 1)
    mate_side, mate_corner = exchange(side, 1), exchange(corner, 1)
    return jnp.concatenate(
        [halves(block, side), halves(mate, mate_side), halves(along, corner), halves(mate_along, mate_corner)],
        axis=1,
    )


def row_total(values):
    return ((values + exchange(values, 1)) + exchange(values, 2)) + exchange(values, 3)


def dot(left, right, left_dim=1, right_dim=0):
    return lax.dot_general(
        left, right, (((left_dim,), (right_dim,)), ((), ())), preferred_element_type=f32
    )


def spread_weight(cut, buffer, put, parts):
    place = lax.axis_index("gx")
    member = lax.axis_index("dp")
    rows = parts // lax.axis_size("dp")
    far = [
        exchange(cut(jnp.bitwise_xor(place, r), member * rows, rows), r) for r in (2, 3)
    ]
    buffer = put(buffer, cut(place, 0, parts), 0, 0)
    buffer = put(buffer, exchange(cut(jnp.bitwise_xor(place, 1), 0, parts), 1), 1, 0)

    def put_both(held, value, index):
        held = put(held, value[0], 2, index * rows)
        return put(held, value[1], 3, index * rows)

    return line_gather(jnp.stack(far), put_both, buffer)


def send_home(pieces):
    pieces = [p.astype(bf16) for p in pieces]
    arrived = [pieces[0]] + [exchange(pieces[r], r) for r in range(1, len(pieces))]
    return in_order([line_sum(p).astype(f32) for p in arrived])


def place_part(part_value, full_shape, offset, axis_dim):
    return lax.dynamic_update_slice_in_dim(jnp.zeros(full_shape, f32), part_value, offset, axis_dim)


def body(
    inputs,
    lengths,
    grad_out,
    gain_mix,
    input_weight,
    branch_weight,
    conv_w,
    conv_b,
    gate_a,
    bias_a,
    gate_x,
    bias_x,
    lam,
    output_weight,
    gain_mlp,
    gate_weight,
    up_weight,
    down_weight,
):
    groups = lax.axis_size("gx")
    column = lax.axis_index("gx")
    length, wide = inputs.shape[1], inputs.shape[2]
    model = wide * groups
    mix_part = input_weight.shape[1] // groups
    feed_part = gate_weight.shape[1] // groups
    block_part = gate_a.shape[0] // groups
    block_size = gate_a.shape[1]
    pitch = pl.cdiv(mix_part, LANES) * LANES
    channel_start = column * mix_part
    block_start = column * block_part
    cols = [slice(r * wide, (r + 1) * wide) for r in range(groups)]

    own = inputs[0]
    far = exchange(own, 2)
    raw = jnp.concatenate([own, exchange(own, 1), far, exchange(far, 1)], axis=1)

    def cut_columns(weight, size):
        return lambda g, start, rows: lax.dynamic_slice(weight, (start, g * size), (rows, size))

    def cut_rows(weight, size):
        return lambda g, start, rows: lax.dynamic_slice(weight, (g * size + start, 0), (rows, weight.shape[1]))

    def put_rows(lane):
        return lambda held, value, r, row: lax.dynamic_update_slice(held, value, (r * wide + row, lane))

    def put_columns(held, value, r, row):
        return lax.dynamic_update_slice(held, value, (row, r * wide))

    joint_weight = jnp.zeros((model, 2 * pitch), bf16)
    joint_weight = spread_weight(cut_columns(input_weight, mix_part), joint_weight, put_rows(0), wide)
    joint_weight = spread_weight(cut_columns(branch_weight, mix_part), joint_weight, put_rows(pitch), wide)
    out_weight = spread_weight(
        cut_rows(output_weight, mix_part), jnp.zeros((mix_part, model), bf16), put_columns, mix_part
    )
    feed_weight = jnp.zeros((model, 2 * feed_part), bf16)
    feed_weight = spread_weight(cut_columns(gate_weight, feed_part), feed_weight, put_rows(0), wide)
    feed_weight = spread_weight(cut_columns(up_weight, feed_part), feed_weight, put_rows(feed_part), wide)
    last_weight = spread_weight(
        cut_rows(down_weight, feed_part), jnp.zeros((feed_part, model), bf16), put_columns, feed_part
    )
    gains = jnp.stack([gain_mix, gain_mlp])
    gains = jnp.concatenate([gains] + [exchange(gains, r) for r in range(1, groups)], axis=1)

    valid_rows = (lax.broadcasted_iota(jnp.int32, (length, 1), 0) < lengths[0]).astype(f32)
    cotangent = grad_out[0]
    far = exchange(cotangent, 2)
    cotangent_full = jnp.concatenate([cotangent, exchange(cotangent, 1), far, exchange(far, 1)], axis=1)
    grad_low = (cotangent_full.astype(f32) * valid_rows).astype(bf16)

    def normalize(values, gain_vec):
        values = values.astype(f32)
        scale_rows = lax.rsqrt(jnp.sum(values * values, axis=1, keepdims=True) / model + norm_eps)
        return (values * scale_rows * gain_vec).astype(bf16), scale_rows

    normed_mix, scale_mix = normalize(raw, gains[0])
    joint = dot(normed_mix, joint_weight)

    def channels(values):
        return lax.dynamic_slice_in_dim(values, channel_start, mix_part, values.ndim - 1)

    def diagonal(blocks):
        blocks = lax.dynamic_slice_in_dim(blocks, block_start, block_part, 0)
        dense = jnp.zeros((mix_part, mix_part), bf16)
        for n in range(block_part):
            dense = lax.dynamic_update_slice(dense, blocks[n], (n * block_size, n * block_size))
        return dense

    taps = channels(conv_w)
    lam_part = channels(lam)[None]
    gate_a_part, gate_x_part = diagonal(gate_a), diagonal(gate_x)
    coef = -decay_power * jax.nn.softplus(-lam_part)
    slope = decay_power * jax.nn.sigmoid(-lam_part)
    mixed, conv_low, sig_a, sig_x, decay, root, state = mixer_forward(
        joint,
        taps,
        channels(conv_b)[None],
        gate_a_part,
        channels(bias_a)[None],
        gate_x_part,
        channels(bias_x)[None],
        coef,
    )
    middle = my_half(own).astype(f32) + plane_scatter([dot(mixed, out_weight[:, c]) for c in cols])

    middle_full = plane_gather(middle.astype(bf16))
    normed_mlp, scale_mlp_full = normalize(middle_full, gains[1])
    feed = dot(normed_mlp, feed_weight)
    gate_value, up_value = feed[:, :feed_part], feed[:, feed_part:]
    grad_hidden = dot(grad_low, last_weight, 1, 1)
    gate_act, gate_slope = gelu_parts(gate_value)
    hidden = (gate_act * up_value).astype(bf16)
    grad_feed = jnp.concatenate(
        [(grad_hidden * up_value * gate_slope).astype(bf16), (grad_hidden * gate_act).astype(bf16)], axis=1
    )
    grad_down = send_home([dot(hidden, grad_low[:, c], 0, 0) for c in cols])
    grad_gate = send_home([dot(normed_mlp[:, c], grad_feed[:, :feed_part], 0, 0) for c in cols])
    grad_up = send_home([dot(normed_mlp[:, c], grad_feed[:, feed_part:], 0, 0) for c in cols])
    grad_normed_mlp = plane_scatter([dot(grad_feed, feed_weight[c], 1, 1) for c in cols])

    unit_mlp = middle * my_half(scale_mlp_full)
    grad_top = my_half(cotangent).astype(f32) * my_half(valid_rows)
    scaled = grad_normed_mlp * gain_mlp
    project = row_total(jnp.sum(scaled * unit_mlp, axis=1)) / model
    grad_middle = grad_top + my_half(scale_mlp_full) * (scaled - unit_mlp * project[:, None])
    gain_mlp_part = jnp.sum(grad_normed_mlp * unit_mlp, axis=0)

    grad_mid_full = plane_gather(grad_middle.astype(bf16))
    grad_mixed = dot(grad_mid_full, out_weight, 1, 1)
    grad_output = send_home([dot(mixed, grad_mid_full[:, c], 0, 0) for c in cols])
    grad_joint, gate_low, input_low, small = mixer_backward(
        grad_mixed, joint, conv_low, sig_a, sig_x, decay, root, state, taps, gate_a_part, gate_x_part, coef, slope
    )
    grad_normed_mix = plane_scatter([dot(grad_joint, joint_weight[c], 1, 1) for c in cols])
    grad_joint_weight = send_home([dot(normed_mix[:, c], grad_joint, 0, 0) for c in cols])

    residual = my_half(own).astype(f32)
    scale_half = my_half(scale_mix)
    unit_mix = residual * scale_half
    scaled = grad_normed_mix * gain_mix
    project = row_total(jnp.sum(scaled * unit_mix, axis=1)) / model
    grad_x = grad_middle + scale_half * (scaled - unit_mix * project[:, None])
    gain_mix_part = jnp.sum(grad_normed_mix * unit_mix, axis=0)

    final = middle + plane_scatter([dot(hidden, last_weight[:, c]) for c in cols])
    output = final.astype(bf16)
    output = halves(output, exchange(output, 0, across=True))[None]
    grad_inputs = grad_x.astype(bf16)
    grad_inputs = halves(grad_inputs, exchange(grad_inputs, 0, across=True))[None]

    gate_blocks = []
    for low in (gate_low, input_low):
        dense = dot(conv_low, low, 0, 0)
        for n in range(block_part):
            span = slice(n * block_size, (n + 1) * block_size)
            gate_blocks.append(dense[span, span])
    gate_blocks = line_sum(jnp.stack(gate_blocks).astype(bf16))
    gate_blocks = in_order([gate_blocks] + [exchange(gate_blocks, r) for r in range(1, groups)])
    gate_blocks = jnp.stack(gate_blocks).astype(f32).reshape(groups, 2, block_part, block_size, block_size)
    grad_gate_a = gate_blocks[:, 0].reshape(gate_a.shape)
    grad_gate_x = gate_blocks[:, 1].reshape(gate_x.shape)
    half_valid = my_half(valid_rows)
    first = jnp.logical_and(column == 0, lax.axis_index("gy") == 0)
    stat_sums = jnp.stack(
        [
            jnp.sum(half_valid * final * final),
            jnp.sum(half_valid * grad_x * grad_x),
            jnp.where(first, jnp.sum(lengths).astype(f32), 0.0),
        ]
    )
    small = lax.psum(place_part(small, (small.shape[0], conv_w.shape[1]), channel_start, 1), ("dp", "gx"))
    grad_gains = lax.psum(jnp.stack([gain_mix_part, gain_mlp_part]), ("dp", "gy"))
    totals = lax.psum(stat_sums, ("dp", "gx", "gy"))
    token_count = totals[2] * model
    taps_count = conv_w.shape[0]

    def joint_columns(start):
        return jnp.concatenate([p[:, start : start + mix_part] for p in grad_joint_weight], axis=1)

    return (
        output,
        grad_inputs,
        grad_gains[0],
        joint_columns(0),
        joint_columns(pitch),
        small[:taps_count],
        small[taps_count],
        grad_gate_a,
        small[taps_count + 1],
        grad_gate_x,
        small[taps_count + 2],
        small[taps_count + 3],
        jnp.concatenate(grad_output, axis=0),
        grad_gains[1],
        jnp.concatenate(grad_gate, axis=1),
        jnp.concatenate(grad_up, axis=1),
        jnp.concatenate(grad_down, axis=0),
        jnp.sqrt(totals[0] / token_count),
        jnp.sqrt(totals[1] / token_count),
    )


def solution(mesh):
    placed = (
        P("dp", None, "gx"),
        P("dp"),
        P("dp", None, "gx"),
        P("gx"),
        P("gx", "gy"),
        P("gx", "gy"),
        P(None, "gy"),
        P("gy"),
        P("gy", None, None),
        P("gy"),
        P("gy", None, None),
        P("gy"),
        P("gy"),
        P("gy", "gx"),
        P("gx"),
        P("gx", "gy"),
        P("gx", "gy"),
        P("gy", "gx"),
    )
    return jax.shard_map(
        body,
        mesh=mesh,
        in_specs=placed,
        out_specs=(
            P("dp", None, "gx"),
            P("dp", None, "gx"),
            P("gx"),
            P("gx", "gy"),
            P("gx", "gy"),
            P(None, "gy"),
            P("gy"),
            P("gy", None, None),
            P("gy"),
            P("gy", None, None),
            P("gy"),
            P("gy"),
            P("gy", "gx"),
            P("gx"),
            P("gx", "gy"),
            P("gx", "gy"),
            P("gy", "gx"),
            P(),
            P(),
        ),
        check_vma=False,
    )
```

time: 3170 us -> 1480 us (0.47)
  waiting for transfers between devices: 1660 us -> 554 us
  local copies, waits for them, and re-layouts: 1090 us -> 146 us
  starting transfers between devices: 1.74 us -> 385 us
  other arithmetic: 158 us -> 80.4 us
  blocking collectives: 99.1 us -> 174 us
  matrix products: 129 us -> 78.3 us
  Pallas kernels: 0 us -> 33.5 us
    psum x5 -> x0, waiting for transfers between devices: 1130 us -> none  [the longest x1 920 us: body(): lax.psum((grad_gain_mix, grad_w_in, grad_w_branch, grad_w_out, grad_gain_...]
    ppermute x0 -> x186, waiting for transfers between devices: none -> 554 us  [the longest x21 154 us: line_sum(): lax.ppermute(value, 'dp', [(s, s + 1), (count - 1 - s, count - 2 - s)])]
    pad x79 -> x0, local copies, waits for them, and re-layouts: 524 us -> none  [linear_state(): return lax.associative_scan(combine, (decay_rate, drive_term), axis=1)[1]]
    slice x76 -> x10, local copies, waits for them, and re-layouts: 516 us -> 9.49 us  [the longest x4 3.38 us: joint_columns(): p[:, start:start + mix_part]]
    ppermute x0 -> x186, starting transfers between devices: none -> 385 us  [the longest x21 168 us: line_sum(): lax.ppermute(value, 'dp', [(s, s + 1), (count - 1 - s, count - 2 - s)])]
    reduce_scatter x6 -> x0, waiting for transfers between devices: 369 us -> none  [the longest x1 102 us: body(): lax.psum_scatter(jnp.dot(normalized_feedforward, up_weight, preferred_ele...]
    all_gather x6 -> x0, waiting for transfers between devices: 167 us -> none  [the longest x1 45 us: body(): hidden_full = lax.all_gather(hidden_activation, 'gx', axis=1, tiled=True)]
    dynamic_update_slice x4 -> x64, local copies, waits for them, and re-layouts: 1.09 us -> 89.6 us  [the longest x39 71 us: put_rows(): lax.dynamic_update_slice(held, value, (r * wide + row, lane))]
  transfers between devices with their start and end apart: 17 -> 186, of which waited for: 15 -> 71; matrix products, arithmetic and copies ran while one was open for 41% -> 17% of each run, Pallas kernels for 0% -> 2%
where the time goes in v1:
time: 1480 us; the launch traced here: 1460 us
  waiting for transfers between devices  554 us (37%)
  starting transfers between devices  385 us (26%)
  blocking collectives  174 us (12%)
  local copies, waits for them, and re-layouts  146 us (10%)
  other arithmetic  80.4 us (5%)
  matrix products  78.3 us (5%)
  Pallas kernels  33.5 us (2%)
    ppermute x21, starting transfers between devices, line_sum(): lax.ppermute(value, 'dp', [(s, s + 1), (count - 1 - s, count - 2 - s)])  168 us
    ppermute x21, waiting for transfers between devices, line_sum(): lax.ppermute(value, 'dp', [(s, s + 1), (count - 1 - s, count - 2 - s)])  154 us
    ppermute x21, waiting for transfers between devices, line_sum(): lax.ppermute(value, 'dp', [(half - 1 - s, half - 2 - s), (half + s, half...  151 us
    ppermute x73, waiting for transfers between devices, exchange(): return lax.ppermute(value, 'gx', [(i, i ^ flip) for i in range(wide)])  90.2 us
    dot_general x42, matrix products, dot(): lax.dot_general(left, right, (((left_dim,), (right_dim,)), ((), ())), pre...  78.3 us
    ppermute x6, waiting for transfers between devices, exchange(): lax.ppermute(value, ('gx', 'gy'), [(i * high + j, (i ^ flip) * high + (j...  75.4 us
    ppermute x18, starting transfers between devices, line_gather(): lax.ppermute(rightward[-1], 'dp', [(i, i + 1) for i in range(count - 1)])  74.3 us
    psum x1, blocking collectives, body(): lax.psum(jnp.stack([gain_mix_part, gain_mlp_part]), ('dp', 'gy'))  72.9 us
  transfers between devices with their start and end apart: 186, of which 71 were waited for; matrix products, arithmetic and copies ran while one was open for 17% of the time, Pallas kernels for 2%

profile of v1, /device:TPU:0, one launch (start us, length us, event | category | flops | bytes accessed | tf_op | source)
XLA Modules:
  0.0 1459.6 jit_solution(627462426728016609)
XLA Ops:
  131.9 11.5 collective-permute-done.12
  294.5 16.4 %collective-permute-done.69 = bf16[2,192,512]{2,1,0:T(8,128)(2,1)S(1)} collective-permute-done((bf16[2,192,512]{2,1,0:T(8,128)(2,1)S(1)}, bf16[2,192,512]{2,1,0:T(8,128)(2,1)S(1)}, u32[]{:S(2)}, u32[]{:S(2)}) %collective-permute-start.69) | collective-permute-done | bytes 393248 | tf_op jit(solution)/shard_map/ppermute | solution.py:296
  338.9 15.2 %mixer_forward.1 = (bf16[1024,352]{1,0:T(8,128)(2,1)S(1)}, bf16[1024,352]{1,0:T(8,128)(2,1)S(1)}, f32[1024,352]{1,0:T(8,128)S(1)}, f32[1024,352]{1,0:T(8,128)S(1...) custom-call(f32[1024,768]{1,0:T(8,128)} %fusion.163.joint_ref, ...), custom_call_target="tpu_custom_call" | custom-call | flops 507510784 | bytes 11534336 | tf_op jit(solution)/shard_map/mixer_forward/pallas_call | solution.py:141
  378.8 9.9 collective-permute-done.37
  392.8 10.2 collective-permute-done.38
  464.7 10.8 collective-permute-done.183
  475.7 16.6 %collective-permute-done.168 = bf16[512,768]{1,0:T(8,128)(2,1)S(1)} collective-permute-done((bf16[512,768]{1,0:T(8,128)(2,1)S(1)}, bf16[512,768]{1,0:T(8,128)(2,1)S(1)}, u32[]{:S(2)}, u32[]{:S(2)}) %collective-permute-start.168) | collective-permute-done | bytes 786464 | tf_op jit(solution)/shard_map/ppermute | solution.py:312
  492.5 15.9 %collective-permute-done.153 = bf16[512,768]{1,0:T(8,128)(2,1)S(1)} collective-permute-done((bf16[512,768]{1,0:T(8,128)(2,1)S(1)}, bf16[512,768]{1,0:T(8,128)(2,1)S(1)}, u32[]{:S(2)}, u32[]{:S(2)}) %collective-permute-start.153) | collective-permute-done | bytes 786464 | tf_op jit(solution)/shard_map/ppermute | solution.py:312
  511.5 16.6 %collective-permute-done.171 = bf16[768,512]{1,0:T(8,128)(2,1)S(1)} collective-permute-done((bf16[768,512]{1,0:T(8,128)(2,1)S(1)}, bf16[768,512]{1,0:T(8,128)(2,1)S(1)}, u32[]{:S(2)}, u32[]{:S(2)}) %collective-permute-start.171) | collective-permute-done | bytes 786464 | tf_op jit(solution)/shard_map/ppermute | solution.py:280
  534.5 9.6 collective-permute-done.175
  561.8 39.4 %collective-permute-done.85 = bf16[512,512]{1,0:T(8,128)(2,1)S(1)} collective-permute-done((bf16[512,512]{1,0:T(8,128)(2,1)S(1)}, bf16[512,512]{1,0:T(8,128)(2,1)S(1)}, u32[]{:S(2)}, u32[]{:S(2)}) %collective-permute-start.85) | collective-permute-done | bytes 524320 | tf_op jit(solution)/shard_map/ppermute | solution.py:283
  611.6 11.8 collective-permute-done.180
  641.2 15.9 %collective-permute-done.161 = bf16[512,768]{1,0:T(8,128)(2,1)S(1)} collective-permute-done((bf16[512,768]{1,0:T(8,128)(2,1)S(1)}, bf16[512,768]{1,0:T(8,128)(2,1)S(1)}, u32[]{:S(2)}, u32[]{:S(2)}) %collective-permute-start.161) | collective-permute-done | bytes 786464 | tf_op jit(solution)/shard_map/ppermute | solution.py:312
  680.0 10.8 collective-permute-done.142
  692.5 15.1 %collective-permute-done.146 = bf16[512,768]{1,0:T(8,128)(2,1)S(1)} collective-permute-done((bf16[512,768]{1,0:T(8,128)(2,1)S(1)}, bf16[512,768]{1,0:T(8,128)(2,1)S(1)}, u32[]{:S(2)}, u32[]{:S(2)}) %collective-permute-start.146) | collective-permute-done | bytes 786464 | tf_op jit(solution)/shard_map/ppermute | solution.py:312
  729.1 10.3 collective-permute-done.93
  750.2 69.4 %collective-permute-start.138 = (bf16[352,512]{1,0:T(8,128)(2,1)S(1)}, bf16[352,512]{1,0:T(8,128)(2,1)S(1)}, u32[]{:S(2)}, u32[]{:S(2)}) collective-permute-start(bf16[352,512]{1,0:T(8,128)(2,1)S(1)} %convolution_convert_fusion.22), channel_id=1, source_target_pairs={{0,8},{24,16},{1,9},{25,17},{2,10},{26,18},{3,11},{27,19},{4,12},{... | collective-permute-start | bytes 1081352 | tf_op jit(solution)/shard_map/ppermute | solution.py:312
  836.7 48.0 %collective-permute-start.131 = (bf16[352,512]{1,0:T(8,128)(2,1)}, bf16[352,512]{1,0:T(8,128)(2,1)}, u32[]{:S(2)}, u32[]{:S(2)}) collective-permute-start(bf16[352,512]{1,0:T(8,128)(2,1)} %collective-permute-done.130), channel_id=1, source_target_pairs={{0,8},{24,16},{1,9},{25,17},{2,10},{26,18},{3,11},{27,19},{4,12},{... | collective-permute-start | bytes 1081352 | tf_op jit(solution)/shard_map/ppermute | solution.py:312
  888.6 18.4 %mixer_backward.1 = (bf16[1024,768]{1,0:T(8,128)(2,1)}, bf16[1024,352]{1,0:T(8,128)(2,1)}, bf16[1024,352]{1,0:T(8,128)(2,1)}, f32[8,352]{1,0:T(8,128)}) custom-call(f32[1024,352]{1,0:T(8,128)} %fusion.6.grad_mixed_ref, f32[1024,768]{1,0:T(8,128)} %fusion.163.joint_ref, bf16[1024,352]{1,0:T(8,128)(2,1)} %copy-done.6, f32[1024,352]{1,0:T(8,128)} %copy-done.2, ...), custom_call_target="tpu_custom_call" | custom-call | flops 507510784 | bytes 14417920 | tf_op jit(solution)/shard_map/mixer_backward/pallas_call | solution.py:258
  929.7 61.5 %psum.22 = f32[8,1408]{1,0:T(8,128)} all-reduce(f32[8,1408]{1,0:T(8,128)} %dynamic_update_slice.259), channel_id=1, replica_groups=mesh['dp'=4,'gx'=4,'gy'=2] {'dp','gx'}, use_global_device_ids=true, to_apply=%region_7.8 | all-reduce | flops 11264 | bytes 90112 | tf_op jit(solution)/shard_map/psum | solution.py:574
  1021.1 19.0 %collective-permute-done.170 = bf16[512,768]{1,0:T(8,128)(2,1)S(1)} collective-permute-done((bf16[512,768]{1,0:T(8,128)(2,1)S(1)}, bf16[512,768]{1,0:T(8,128)(2,1)S(1)}, u32[]{:S(2)}, u32[]{:S(2)}) %collective-permute-start.170) | collective-permute-done | bytes 786464 | tf_op jit(solution)/shard_map/ppermute | solution.py:317
  1041.4 32.4 %collective-permute-done.159 = bf16[512,768]{1,0:T(8,128)(2,1)S(1)} collective-permute-done((bf16[512,768]{1,0:T(8,128)(2,1)S(1)}, bf16[512,768]{1,0:T(8,128)(2,1)S(1)}, u32[]{:S(2)}, u32[]{:S(2)}) %collective-permute-start.159) | collective-permute-done | bytes 786464 | tf_op jit(solution)/shard_map/ppermute | solution.py:317
  1075.1 15.6 %collective-permute-done.163 = bf16[512,768]{1,0:T(8,128)(2,1)S(1)} collective-permute-done((bf16[512,768]{1,0:T(8,128)(2,1)S(1)}, bf16[512,768]{1,0:T(8,128)(2,1)S(1)}, u32[]{:S(2)}, u32[]{:S(2)}) %collective-permute-start.163) | collective-permute-done | bytes 786464 | tf_op jit(solution)/shard_map/ppermute | solution.py:317
  1092.0 15.6 %collective-permute-done.167 = bf16[512,768]{1,0:T(8,128)(2,1)S(1)} collective-permute-done((bf16[512,768]{1,0:T(8,128)(2,1)S(1)}, bf16[512,768]{1,0:T(8,128)(2,1)S(1)}, u32[]{:S(2)}, u32[]{:S(2)}) %collective-permute-start.167) | collective-permute-done | bytes 786464 | tf_op jit(solution)/shard_map/ppermute | solution.py:317
  1124.4 16.8 %collective-permute-done.148 = bf16[512,768]{1,0:T(8,128)(2,1)S(1)} collective-permute-done((bf16[512,768]{1,0:T(8,128)(2,1)S(1)}, bf16[512,768]{1,0:T(8,128)(2,1)S(1)}, u32[]{:S(2)}, u32[]{:S(2)}) %collective-permute-start.148) | collective-permute-done | bytes 786464 | tf_op jit(solution)/shard_map/ppermute | solution.py:317
  1162.0 16.8 %collective-permute-done.135 = bf16[352,512]{1,0:T(8,128)(2,1)S(1)} collective-permute-done((bf16[352,512]{1,0:T(8,128)(2,1)S(1)}, bf16[352,512]{1,0:T(8,128)(2,1)S(1)}, u32[]{:S(2)}, u32[]{:S(2)}) %collective-permute-start.135) | collective-permute-done | bytes 360480 | tf_op jit(solution)/shard_map/ppermute | solution.py:312
  1178.9 9.1 collective-permute-start.123
  1216.7 13.7 collective-permute-done.140
  1270.0 10.1 collective-permute-done.99
  1286.3 12.1 collective-permute-done.114
  1318.9 72.9 %psum.21 = f32[2,512]{1,0:T(2,128)S(1)} all-reduce(f32[2,512]{1,0:T(2,128)S(1)} %pad_maximum_fusion.16), channel_id=1, replica_groups=mesh['dp'=4,'gx'=4,'gy'=2] {'dp','gy'}, use_global_device_ids=true, to_apply=%region_6.7 | all-reduce | flops 1024 | bytes 8192 | tf_op jit(solution)/shard_map/psum | solution.py:575
  1394.2 39.4 %psum.23 = f32[3]{0:T(128)S(1)} all-reduce(f32[3]{0:T(128)S(1)} %pad_maximum_fusion.17), channel_id=1, replica_groups=mesh['dp'=4,'gx'=4,'gy'=2] {'dp','gx','gy'}, use_global_device_ids=true, to_apply=%region_10.11 | all-reduce | flops 3 | bytes 24 | tf_op jit(solution)/shard_map/psum | solution.py:576
  (791 shorter events, 743.9 us)
Async XLA Ops:
  80.0 130.2 %collective-permute-start.15 = (bf16[512,352]{1,0:T(8,128)(2,1)}, bf16[512,352]{1,0:T(8,128)(2,1)}, u32[]{:S(2)}, u32[]{:S(2)}) collective-permute-start(bf16[512,352]{1,0:T(8,128)(2,1)} %get-tuple-element.134), channel_id=1, source_target_pairs={{0,2},{2,0},{4,6},{6,4},{1,3},{3,1},{5,7},{7,5},{8,10},{10,8},{12,... | collective-permute-start | bytes 1081352 | tf_op jit(solution)/shard_map/ppermute | solution.py:280
  119.2 124.9 %collective-permute-start.45 = (bf16[512,768]{1,0:T(8,128)(2,1)}, bf16[512,768]{1,0:T(8,128)(2,1)}, u32[]{:S(2)}, u32[]{:S(2)}) collective-permute-start(bf16[512,768]{1,0:T(8,128)(2,1)} %get-tuple-element.109), channel_id=1, source_target_pairs={{0,2},{2,0},{4,6},{6,4},{1,3},{3,1},{5,7},{7,5},{8,10},{10,8},{12,... | collective-permute-start | bytes 2359304 | tf_op jit(solution)/shard_map/ppermute | solution.py:280
  119.3 135.7 %collective-permute-start.63 = (bf16[768,512]{1,0:T(8,128)(2,1)}, bf16[768,512]{1,0:T(8,128)(2,1)S(1)}, u32[]{:S(2)}, u32[]{:S(2)}) collective-permute-start(bf16[768,512]{1,0:T(8,128)(2,1)} %get-tuple-element.101), channel_id=1, source_target_pairs={{0,2},{2,0},{4,6},{6,4},{1,3},{3,1},{5,7},{7,5},{8,10},{10,8},{12,... | collective-permute-start | bytes 2359304 | tf_op jit(solution)/shard_map/ppermute | solution.py:280
  128.4 111.0 %collective-permute-start.49 = (bf16[2,128,768]{2,1,0:T(8,128)(2,1)}, bf16[2,128,768]{2,1,0:T(8,128)(2,1)}, u32[]{:S(2)}, u32[]{:S(2)}) collective-permute-start(bf16[2,128,768]{2,1,0:T(8,128)(2,1)} %pad_maximum_fusion.7), channel_id=1, source_target_pairs={{8,0},{16,8},{24,16},{9,1},{17,9},{25,17},{10,2},{18,10},{26,18},{... | collective-permute-start | bytes 1179656 | tf_op jit(solution)/shard_map/ppermute | solution.py:296
  181.3 67.9 %collective-permute-start.48 = (bf16[2,128,768]{2,1,0:T(8,128)(2,1)}, bf16[2,128,768]{2,1,0:T(8,128)(2,1)}, u32[]{:S(2)}, u32[]{:S(2)}) collective-permute-start(bf16[2,128,768]{2,1,0:T(8,128)(2,1)} %pad_maximum_fusion.7), channel_id=1, source_target_pairs={{0,8},{8,16},{16,24},{1,9},{9,17},{17,25},{2,10},{10,18},{18,26},{... | collective-permute-start | bytes 1179656 | tf_op jit(solution)/shard_map/ppermute | solution.py:295
  452.6 79.0 %collective-permute-start.72 = (bf16[1024,512]{1,0:T(8,128)(2,1)S(1)}, bf16[1024,512]{1,0:T(8,128)(2,1)S(1)}, u32[]{:S(2)}, u32[]{:S(2)}) collective-permute-start(bf16[1024,512]{1,0:T(8,128)(2,1)S(1)} %convolution_convert_fusion.3), channel_id=1, source_target_pairs={{0,2},{2,0},{4,6},{6,4},{1,3},{3,1},{5,7},{7,5},{8,10},{10,8},{12,... | collective-permute-start | bytes 3145736 | tf_op jit(solution)/shard_map/ppermute | solution.py:280
  475.4 71.3 %collective-permute-start.74 = (bf16[1024,512]{1,0:T(8,128)(2,1)S(1)}, bf16[1024,512]{1,0:T(8,128)(2,1)S(1)}, u32[]{:S(2)}, u32[]{:S(2)}) collective-permute-start(bf16[1024,512]{1,0:T(8,128)(2,1)S(1)} %convolution_convert_fusion.2), channel_id=1, source_target_pairs={{0,2},{2,0},{4,6},{6,4},{1,3},{3,1},{5,7},{7,5},{8,10},{10,8},{12,... | collective-permute-start | bytes 3145736 | tf_op jit(solution)/shard_map/ppermute | solution.py:280
  544.2 62.0 %collective-permute-start.156 = (bf16[512,768]{1,0:T(8,128)(2,1)S(1)}, bf16[512,768]{1,0:T(8,128)(2,1)S(1)}, u32[]{:S(2)}, u32[]{:S(2)}) collective-permute-start(bf16[512,768]{1,0:T(8,128)(2,1)S(1)} %convolution_convert_fusion.13), channel_id=1, source_target_pairs={{0,6},{2,4},{4,2},{6,0},{1,7},{3,5},{5,3},{7,1},{8,14},{10,12},{12... | collective-permute-start | bytes 2359304 | tf_op jit(solution)/shard_map/ppermute | solution.py:280
  661.8 63.6 %collective-permute-start.154 = (bf16[512,768]{1,0:T(8,128)(2,1)S(1)}, bf16[512,768]{1,0:T(8,128)(2,1)S(1)}, u32[]{:S(2)}, u32[]{:S(2)}) collective-permute-start(bf16[512,768]{1,0:T(8,128)(2,1)S(1)} %add_convert_fusion.21), channel_id=1, source_target_pairs={{8,16},{16,8},{9,17},{17,9},{10,18},{18,10},{11,19},{19,11},{12,20... | collective-permute-start | bytes 2359304 | tf_op jit(solution)/shard_map/ppermute | solution.py:314
  743.6 77.1 %collective-permute-start.143 = (bf16[512,768]{1,0:T(8,128)(2,1)S(1)}, bf16[512,768]{1,0:T(8,128)(2,1)S(1)}, u32[]{:S(2)}, u32[]{:S(2)}) collective-permute-start(bf16[512,768]{1,0:T(8,128)(2,1)S(1)} %add_convert_fusion.27), channel_id=1, source_target_pairs={{8,16},{16,8},{9,17},{17,9},{10,18},{18,10},{11,19},{19,11},{12,20... | collective-permute-start | bytes 2359304 | tf_op jit(solution)/shard_map/ppermute | solution.py:314
  745.4 76.4 %collective-permute-start.147 = (bf16[512,768]{1,0:T(8,128)(2,1)S(1)}, bf16[512,768]{1,0:T(8,128)(2,1)S(1)}, u32[]{:S(2)}, u32[]{:S(2)}) collective-permute-start(bf16[512,768]{1,0:T(8,128)(2,1)S(1)} %add_convert_fusion.25), channel_id=1, source_target_pairs={{8,16},{16,8},{9,17},{17,9},{10,18},{18,10},{11,19},{19,11},{12,20... | collective-permute-start | bytes 2359304 | tf_op jit(solution)/shard_map/ppermute | solution.py:314
  747.3 76.1 %collective-permute-start.151 = (bf16[512,768]{1,0:T(8,128)(2,1)S(1)}, bf16[512,768]{1,0:T(8,128)(2,1)S(1)}, u32[]{:S(2)}, u32[]{:S(2)}) collective-permute-start(bf16[512,768]{1,0:T(8,128)(2,1)S(1)} %add_convert_fusion.23), channel_id=1, source_target_pairs={{8,16},{16,8},{9,17},{17,9},{10,18},{18,10},{11,19},{19,11},{12,20... | collective-permute-start | bytes 2359304 | tf_op jit(solution)/shard_map/ppermute | solution.py:314
  749.1 79.3 %collective-permute-start.90 = (bf16[512,512]{1,0:T(8,128)(2,1)S(1)}, bf16[512,512]{1,0:T(8,128)(2,1)S(1)}, u32[]{:S(2)}, u32[]{:S(2)}) collective-permute-start(bf16[512,512]{1,0:T(8,128)(2,1)S(1)} %get-tuple-element.79), channel_id=1, source_target_pairs={{0,2},{2,0},{4,6},{6,4},{1,3},{3,1},{5,7},{7,5},{8,10},{10,8},{12,... | collective-permute-start | bytes 1572872 | tf_op jit(solution)/shard_map/ppermute | solution.py:280
  750.2 75.8 %collective-permute-start.138 = (bf16[352,512]{1,0:T(8,128)(2,1)S(1)}, bf16[352,512]{1,0:T(8,128)(2,1)S(1)}, u32[]{:S(2)}, u32[]{:S(2)}) collective-permute-start(bf16[352,512]{1,0:T(8,128)(2,1)S(1)} %convolution_convert_fusion.22), channel_id=1, source_target_pairs={{0,8},{24,16},{1,9},{25,17},{2,10},{26,18},{3,11},{27,19},{4,12},{... | collective-permute-start | bytes 1081352 | tf_op jit(solution)/shard_map/ppermute | solution.py:312
  828.4 173.5 %collective-permute-start.185 = (bf16[768,512]{1,0:T(8,128)(2,1)}, bf16[768,512]{1,0:T(8,128)(2,1)}, u32[]{:S(2)}, u32[]{:S(2)}) collective-permute-start(bf16[768,512]{1,0:T(8,128)(2,1)} %add_convert_fusion.4), channel_id=1, source_target_pairs={{8,0},{16,24},{9,1},{17,25},{10,2},{18,26},{11,3},{19,27},{12,4},{... | collective-permute-start | bytes 2359304 | tf_op jit(solution)/shard_map/ppermute | solution.py:317
  829.7 173.6 %collective-permute-start.174 = (bf16[768,512]{1,0:T(8,128)(2,1)}, bf16[768,512]{1,0:T(8,128)(2,1)}, u32[]{:S(2)}, u32[]{:S(2)}) collective-permute-start(bf16[768,512]{1,0:T(8,128)(2,1)} %add_convert_fusion.10), channel_id=1, source_target_pairs={{8,0},{16,24},{9,1},{17,25},{10,2},{18,26},{11,3},{19,27},{12,4},{... | collective-permute-start | bytes 2359304 | tf_op jit(solution)/shard_map/ppermute | solution.py:317
  835.4 169.2 %collective-permute-start.178 = (bf16[768,512]{1,0:T(8,128)(2,1)}, bf16[768,512]{1,0:T(8,128)(2,1)}, u32[]{:S(2)}, u32[]{:S(2)}) collective-permute-start(bf16[768,512]{1,0:T(8,128)(2,1)} %add_convert_fusion.8), channel_id=1, source_target_pairs={{8,0},{16,24},{9,1},{17,25},{10,2},{18,26},{11,3},{19,27},{12,4},{... | collective-permute-start | bytes 2359304 | tf_op jit(solution)/shard_map/ppermute | solution.py:317
  836.7 159.4 %collective-permute-start.131 = (bf16[352,512]{1,0:T(8,128)(2,1)}, bf16[352,512]{1,0:T(8,128)(2,1)}, u32[]{:S(2)}, u32[]{:S(2)}) collective-permute-start(bf16[352,512]{1,0:T(8,128)(2,1)} %collective-permute-done.130), channel_id=1, source_target_pairs={{0,8},{24,16},{1,9},{25,17},{2,10},{26,18},{3,11},{27,19},{4,12},{... | collective-permute-start | bytes 1081352 | tf_op jit(solution)/shard_map/ppermute | solution.py:312
  926.4 71.3 %collective-permute-start.120 = (bf16[4,176,176]{2,1,0:T(8,128)(2,1)}, bf16[4,176,176]{2,1,0:T(8,128)(2,1)S(1)}, u32[]{:S(2)}, u32[]{:S(2)}) collective-permute-start(bf16[4,176,176]{2,1,0:T(8,128)(2,1)} %pad_maximum_fusion.10), channel_id=1, source_target_pairs={{0,8},{24,16},{1,9},{25,17},{2,10},{26,18},{3,11},{27,19},{4,12},{... | collective-permute-start | bytes 743432 | tf_op jit(solution)/shard_map/ppermute | solution.py:312
  1002.0 110.2 %collective-permute-start.155 = (bf16[512,768]{1,0:T(8,128)(2,1)S(1)}, bf16[512,768]{1,0:T(8,128)(2,1)S(1)}, u32[]{:S(2)}, u32[]{:S(2)}) collective-permute-start(bf16[512,768]{1,0:T(8,128)(2,1)S(1)} %copy-done.17), channel_id=1, source_target_pairs={{8,0},{16,24},{9,1},{17,25},{10,2},{18,26},{11,3},{19,27},{12,4},{... | collective-permute-start | bytes 2359304 | tf_op jit(solution)/shard_map/ppermute | solution.py:317
  1003.3 70.5 %collective-permute-start.159 = (bf16[512,768]{1,0:T(8,128)(2,1)S(1)}, bf16[512,768]{1,0:T(8,128)(2,1)S(1)}, u32[]{:S(2)}, u32[]{:S(2)}) collective-permute-start(bf16[512,768]{1,0:T(8,128)(2,1)S(1)} %copy-done.21), channel_id=1, source_target_pairs={{8,0},{16,24},{9,1},{17,25},{10,2},{18,26},{11,3},{19,27},{12,4},{... | collective-permute-start | bytes 2359304 | tf_op jit(solution)/shard_map/ppermute | solution.py:317
  1004.6 86.0 %collective-permute-start.163 = (bf16[512,768]{1,0:T(8,128)(2,1)S(1)}, bf16[512,768]{1,0:T(8,128)(2,1)S(1)}, u32[]{:S(2)}, u32[]{:S(2)}) collective-permute-start(bf16[512,768]{1,0:T(8,128)(2,1)S(1)} %copy-done.22), channel_id=1, source_target_pairs={{8,0},{16,24},{9,1},{17,25},{10,2},{18,26},{11,3},{19,27},{12,4},{... | collective-permute-start | bytes 2359304 | tf_op jit(solution)/shard_map/ppermute | solution.py:317
  1013.2 94.3 %collective-permute-start.167 = (bf16[512,768]{1,0:T(8,128)(2,1)S(1)}, bf16[512,768]{1,0:T(8,128)(2,1)S(1)}, u32[]{:S(2)}, u32[]{:S(2)}) collective-permute-start(bf16[512,768]{1,0:T(8,128)(2,1)S(1)} %copy-done.23), channel_id=1, source_target_pairs={{8,0},{16,24},{9,1},{17,25},{10,2},{18,26},{11,3},{19,27},{12,4},{... | collective-permute-start | bytes 2359304 | tf_op jit(solution)/shard_map/ppermute | solution.py:317
  1040.1 84.3 %collective-permute-start.144 = (bf16[512,768]{1,0:T(8,128)(2,1)S(1)}, bf16[512,768]{1,0:T(8,128)(2,1)S(1)}, u32[]{:S(2)}, u32[]{:S(2)}) collective-permute-start(bf16[512,768]{1,0:T(8,128)(2,1)S(1)} %copy-done.18), channel_id=1, source_target_pairs={{8,0},{16,24},{9,1},{17,25},{10,2},{18,26},{11,3},{19,27},{12,4},{... | collective-permute-start | bytes 2359304 | tf_op jit(solution)/shard_map/ppermute | solution.py:317
  1073.8 67.4 %collective-permute-start.148 = (bf16[512,768]{1,0:T(8,128)(2,1)S(1)}, bf16[512,768]{1,0:T(8,128)(2,1)S(1)}, u32[]{:S(2)}, u32[]{:S(2)}) collective-permute-start(bf16[512,768]{1,0:T(8,128)(2,1)S(1)} %copy-done.19), channel_id=1, source_target_pairs={{8,0},{16,24},{9,1},{17,25},{10,2},{18,26},{11,3},{19,27},{12,4},{... | collective-permute-start | bytes 2359304 | tf_op jit(solution)/shard_map/ppermute | solution.py:317
  1112.2 99.2 %collective-permute-start.96 = (bf16[1024,512]{1,0:T(8,128)(2,1)S(1)}, bf16[1024,512]{1,0:T(8,128)(2,1)S(1)}, u32[]{:S(2)}, u32[]{:S(2)}) collective-permute-start(bf16[1024,512]{1,0:T(8,128)(2,1)S(1)} %copy-done.79), channel_id=1, source_target_pairs={{0,2},{2,0},{4,6},{6,4},{1,3},{3,1},{5,7},{7,5},{8,10},{10,8},{12,... | collective-permute-start | bytes 3145736 | tf_op jit(solution)/shard_map/ppermute | solution.py:280
  1118.1 113.6 %collective-permute-start.98 = (bf16[1024,512]{1,0:T(8,128)(2,1)S(1)}, bf16[1024,512]{1,0:T(8,128)(2,1)S(1)}, u32[]{:S(2)}, u32[]{:S(2)}) collective-permute-start(bf16[1024,512]{1,0:T(8,128)(2,1)S(1)} %copy-done.78), channel_id=1, source_target_pairs={{0,2},{2,0},{4,6},{6,4},{1,3},{3,1},{5,7},{7,5},{8,10},{10,8},{12,... | collective-permute-start | bytes 3145736 | tf_op jit(solution)/shard_map/ppermute | solution.py:280
  1308.7 133.0 %collective-permute-start.119 = (bf16[512,768]{1,0:T(8,128)(2,1)S(1)}, bf16[512,768]{1,0:T(8,128)(2,1)}, u32[]{:S(2)}, u32[]{:S(2)}) collective-permute-start(bf16[512,768]{1,0:T(8,128)(2,1)S(1)} %add_convert_fusion.28), channel_id=1, source_target_pairs={{8,0},{16,24},{9,1},{17,25},{10,2},{18,26},{11,3},{19,27},{12,4},{... | collective-permute-start | bytes 2359304 | tf_op jit(solution)/shard_map/ppermute | solution.py:317
  1313.2 78.6 %collective-permute-start.104 = (bf16[512,512]{1,0:T(8,128)(2,1)}, bf16[512,512]{1,0:T(8,128)(2,1)}, u32[]{:S(2)}, u32[]{:S(2)}) collective-permute-start(bf16[512,512]{1,0:T(8,128)(2,1)} %get-tuple-element.51), channel_id=1, source_target_pairs={{0,1},{1,0},{2,3},{3,2},{4,5},{5,4},{6,7},{7,6},{8,9},{9,8},{10,11... | collective-permute-start | bytes 1572872 | tf_op jit(solution)/shard_map/ppermute | solution.py:282
  1314.6 127.1 %collective-permute-start.112 = (bf16[512,768]{1,0:T(8,128)(2,1)S(1)}, bf16[512,768]{1,0:T(8,128)(2,1)}, u32[]{:S(2)}, u32[]{:S(2)}) collective-permute-start(bf16[512,768]{1,0:T(8,128)(2,1)S(1)} %add_convert_fusion.32), channel_id=1, source_target_pairs={{8,0},{16,24},{9,1},{17,25},{10,2},{18,26},{11,3},{19,27},{12,4},{... | collective-permute-start | bytes 2359304 | tf_op jit(solution)/shard_map/ppermute | solution.py:317
  1316.1 125.6 %collective-permute-start.108 = (bf16[512,768]{1,0:T(8,128)(2,1)S(1)}, bf16[512,768]{1,0:T(8,128)(2,1)}, u32[]{:S(2)}, u32[]{:S(2)}) collective-permute-start(bf16[512,768]{1,0:T(8,128)(2,1)S(1)} %add_convert_fusion.34), channel_id=1, source_target_pairs={{8,0},{16,24},{9,1},{17,25},{10,2},{18,26},{11,3},{19,27},{12,4},{... | collective-permute-start | bytes 2359304 | tf_op jit(solution)/shard_map/ppermute | solution.py:317
  1317.6 124.1 %collective-permute-start.116 = (bf16[512,768]{1,0:T(8,128)(2,1)S(1)}, bf16[512,768]{1,0:T(8,128)(2,1)}, u32[]{:S(2)}, u32[]{:S(2)}) collective-permute-start(bf16[512,768]{1,0:T(8,128)(2,1)S(1)} %add_convert_fusion.30), channel_id=1, source_target_pairs={{8,0},{16,24},{9,1},{17,25},{10,2},{18,26},{11,3},{19,27},{12,4},{... | collective-permute-start | bytes 2359304 | tf_op jit(solution)/shard_map/ppermute | solution.py:317
  (240 other events, 6133.1 us)

commit v2 on v1

--- a/solution.py
+++ b/solution.py
@@ -287,18 +287,8 @@
     )
 
 
-def line_gather(value, place, buffer):
-    count = lax.axis_size("dp")
-    here = lax.axis_index("dp")
-    rightward, leftward = [value], [value]
-    for _ in range(count - 1):
-        rightward.append(lax.ppermute(rightward[-1], "dp", [(i, i + 1) for i in range(count - 1)]))
-        leftward.append(lax.ppermute(leftward[-1], "dp", [(i + 1, i) for i in range(count - 1)]))
-    buffer = place(buffer, value, here)
-    for s in range(1, count):
-        arrived = jnp.where(here >= s, rightward[s], leftward[count - s])
-        buffer = place(buffer, arrived, jnp.where(here >= s, here - s, here - s + count))
-    return buffer
+def after(value, *earlier):
+    return lax.optimization_barrier((value,) + earlier)[0] if earlier else value
 
 
 def line_sum(value):
@@ -306,36 +296,31 @@
     here = lax.axis_index("dp")
     kind = value.dtype
     if count == 1:
-        return value
+        return value, value
     half = count // 2
+    first = None
     for s in range(half - 1):
         arrived = lax.ppermute(value, "dp", [(s, s + 1), (count - 1 - s, count - 2 - s)])
+        first = arrived if first is None else first
         value = (value.astype(f32) + arrived.astype(f32)).astype(kind)
     arrived = lax.ppermute(value, "dp", [(half - 1, half), (half, half - 1)])
+    first = arrived if first is None else first
     value = (value.astype(f32) + arrived.astype(f32)).astype(kind)
     for s in range(half - 1):
         arrived = lax.ppermute(value, "dp", [(half - 1 - s, half - 2 - s), (half + s, half + s + 1)])
         takes = jnp.logical_or(here == half - 2 - s, here == half + s + 1)
         value = jnp.where(takes, arrived, value)
-    return value
-
-
-def in_order(pieces):
-    place = lax.axis_index("gx")
-    count = len(pieces)
-    bit = 1
-    while bit < count:
-        swapped = jnp.bitwise_and(place, bit) != 0
-        pieces = [jnp.where(swapped, pieces[r ^ bit], pieces[r]) for r in range(count)]
-        bit *= 2
-    return pieces
+    return value, first
+
+
+def joined(mine, other, mine_first, axis=0):
+    return jnp.where(
+        mine_first, jnp.concatenate([mine, other], axis=axis), jnp.concatenate([other, mine], axis=axis)
+    )
 
 
 def halves(mine, other):
-    side = lax.axis_index("gy")
-    return jnp.where(
-        side == 0, jnp.concatenate([mine, other], axis=0), jnp.concatenate([other, mine], axis=0)
-    )
+    return joined(mine, other, lax.axis_index("gy") == 0)
 
 
 def my_half(values, other=False):
@@ -344,28 +329,31 @@
     return lax.dynamic_slice_in_dim(values, ((1 - side) if other else side) * rows, rows, 0)
 
 
-def plane_scatter(pieces):
-    low = [p.astype(bf16) for p in pieces]
-    kept = pieces[0] + exchange(low[1], 1).astype(f32)
-    passed = (pieces[2] + exchange(low[3], 1).astype(f32)).astype(bf16)
+def widen(own):
+    near = exchange(my_half(own), 2)
+    even = jnp.concatenate([own, halves(near, exchange(near, 0, across=True))], axis=1)
+    return even, exchange(even, 1)
+
+
+def plane_scatter(even, odd):
+    wide = even.shape[1] // 2
+    total = even + exchange(odd.astype(bf16), 1).astype(f32)
+    kept, passed = total[:, :wide], total[:, wide:].astype(bf16)
+    along = exchange(my_half(passed), 2)
     side = exchange(my_half(kept, other=True).astype(bf16), 0, across=True)
-    along = exchange(my_half(passed), 2)
     corner = exchange(my_half(passed, other=True), 2, across=True)
     return (my_half(kept) + side.astype(f32)) + (along.astype(f32) + corner.astype(f32))
 
 
 def plane_gather(block):
     along, side, corner = exchange(block, 2), exchange(block, 0, across=True), exchange(block, 2, across=True)
-    mate, mate_along = exchange(block, 1), exchange(along, 1)
-    mate_side, mate_corner = exchange(side, 1), exchange(corner, 1)
-    return jnp.concatenate(
-        [halves(block, side), halves(mate, mate_side), halves(along, corner), halves(mate_along, mate_corner)],
-        axis=1,
-    )
+    even = halves(jnp.concatenate([block, along], axis=1), jnp.concatenate([side, corner], axis=1))
+    return jnp.concatenate([even, exchange(even, 1)], axis=1), along
 
 
 def row_total(values):
-    return ((values + exchange(values, 1)) + exchange(values, 2)) + exchange(values, 3)
+    values = values + exchange(values, 1)
+    return values + exchange(values, 2)
 
 
 def dot(left, right, left_dim=1, right_dim=0):
@@ -374,31 +362,38 @@
     )
 
 
-def spread_weight(cut, buffer, put, parts):
+def from_neighbour(own, far):
+    if lax.axis_size("dp") % 2:
+        return exchange(far, 2), None
+    near = exchange(far, 2)
+    member = lax.axis_index("dp")
+    pairs = [(i, i ^ 1) for i in range(lax.axis_size("dp"))]
+    return near, lambda value: joined(value, lax.ppermute(value, "dp", pairs), member % 2 == 0)
+
+
+def chip_cut(weight, axis, neighbour):
+    size = 2 * (weight.shape[axis] // lax.axis_size("gx"))
+    place = lax.axis_index("gx") // 2
+    return lax.dynamic_slice_in_dim(weight, ((1 - place) if neighbour else place) * size, size, axis)
+
+
+def dp_half(values):
+    if lax.axis_size("dp") % 2:
+        return values
+    rows = values.shape[0] // 2
+    return lax.dynamic_slice_in_dim(values, (lax.axis_index("dp") % 2) * rows, rows, 0)
+
+
+def core_cut(values, axis, mate):
+    size = values.shape[axis] // 2
+    core = lax.axis_index("gx") % 2
+    return lax.dynamic_slice_in_dim(values, ((1 - core) if mate else core) * size, size, axis)
+
+
+def in_order(own, mate, near, near_mate, axis):
     place = lax.axis_index("gx")
-    member = lax.axis_index("dp")
-    rows = parts // lax.axis_size("dp")
-    far = [
-        exchange(cut(jnp.bitwise_xor(place, r), member * rows, rows), r) for r in (2, 3)
-    ]
-    buffer = put(buffer, cut(place, 0, parts), 0, 0)
-    buffer = put(buffer, exchange(cut(jnp.bitwise_xor(place, 1), 0, parts), 1), 1, 0)
-
-    def put_both(held, value, index):
-        held = put(held, value[0], 2, index * rows)
-        return put(held, value[1], 3, index * rows)
-
-    return line_gather(jnp.stack(far), put_both, buffer)
-
-
-def send_home(pieces):
-    pieces = [p.astype(bf16) for p in pieces]
-    arrived = [pieces[0]] + [exchange(pieces[r], r) for r in range(1, len(pieces))]
-    return in_order([line_sum(p).astype(f32) for p in arrived])
-
-
-def place_part(part_value, full_shape, offset, axis_dim):
-    return lax.dynamic_update_slice_in_dim(jnp.zeros(full_shape, f32), part_value, offset, axis_dim)
+    core_first, chip_first = place % 2 == 0, place // 2 == 0
+    return joined(joined(own, mate, core_first, axis), joined(near, near_mate, core_first, axis), chip_first, axis)
 
 
 def body(
@@ -425,6 +420,7 @@
     column = lax.axis_index("gx")
     length, wide = inputs.shape[1], inputs.shape[2]
     model = wide * groups
+    half = model // 2
     mix_part = input_weight.shape[1] // groups
     feed_part = gate_weight.shape[1] // groups
     block_part = gate_a.shape[0] // groups
@@ -432,51 +428,49 @@
     pitch = pl.cdiv(mix_part, LANES) * LANES
     channel_start = column * mix_part
     block_start = column * block_part
-    cols = [slice(r * wide, (r + 1) * wide) for r in range(groups)]
-
     own = inputs[0]
-    far = exchange(own, 2)
-    raw = jnp.concatenate([own, exchange(own, 1), far, exchange(far, 1)], axis=1)
-
-    def cut_columns(weight, size):
-        return lambda g, start, rows: lax.dynamic_slice(weight, (start, g * size), (rows, size))
-
-    def cut_rows(weight, size):
-        return lambda g, start, rows: lax.dynamic_slice(weight, (g * size + start, 0), (rows, weight.shape[1]))
-
-    def put_rows(lane):
-        return lambda held, value, r, row: lax.dynamic_update_slice(held, value, (r * wide + row, lane))
-
-    def put_columns(held, value, r, row):
-        return lax.dynamic_update_slice(held, value, (row, r * wide))
-
-    joint_weight = jnp.zeros((model, 2 * pitch), bf16)
-    joint_weight = spread_weight(cut_columns(input_weight, mix_part), joint_weight, put_rows(0), wide)
-    joint_weight = spread_weight(cut_columns(branch_weight, mix_part), joint_weight, put_rows(pitch), wide)
-    out_weight = spread_weight(
-        cut_rows(output_weight, mix_part), jnp.zeros((mix_part, model), bf16), put_columns, mix_part
-    )
-    feed_weight = jnp.zeros((model, 2 * feed_part), bf16)
-    feed_weight = spread_weight(cut_columns(gate_weight, feed_part), feed_weight, put_rows(0), wide)
-    feed_weight = spread_weight(cut_columns(up_weight, feed_part), feed_weight, put_rows(feed_part), wide)
-    last_weight = spread_weight(
-        cut_rows(down_weight, feed_part), jnp.zeros((feed_part, model), bf16), put_columns, feed_part
-    )
+
+    def far_columns(weights):
+        return jnp.concatenate([dp_half(chip_cut(w, 1, True)) for w in weights], axis=1)
+
+    joint_far, joint_fill = from_neighbour(None, far_columns([input_weight, branch_weight]))
+    raw_even, raw_odd = widen(own)
+    out_far, out_fill = from_neighbour(None, dp_half(chip_cut(output_weight, 0, True)))
+    feed_far, feed_fill = from_neighbour(None, far_columns([gate_weight, up_weight]))
+    last_far, last_fill = from_neighbour(None, dp_half(chip_cut(down_weight, 0, True)))
     gains = jnp.stack([gain_mix, gain_mlp])
-    gains = jnp.concatenate([gains] + [exchange(gains, r) for r in range(1, groups)], axis=1)
-
-    valid_rows = (lax.broadcasted_iota(jnp.int32, (length, 1), 0) < lengths[0]).astype(f32)
-    cotangent = grad_out[0]
-    far = exchange(cotangent, 2)
-    cotangent_full = jnp.concatenate([cotangent, exchange(cotangent, 1), far, exchange(far, 1)], axis=1)
-    grad_low = (cotangent_full.astype(f32) * valid_rows).astype(bf16)
+    gains = jnp.concatenate([gains, exchange(gains, 2)], axis=1)
+    gains = jnp.concatenate([gains, exchange(gains, 1)], axis=1)
+
+    def fill(far, filler):
+        return filler(far) if filler is not None else far
+
+    def column_weight(weights, far, filler, pitch):
+        far = fill(far, filler)
+        near = jnp.concatenate([chip_cut(w, 1, False) for w in weights], axis=1)
+        both = jnp.concatenate([near, far], axis=0)
+        size = both.shape[1] // len(weights)
+
+        def cut(mate):
+            parts = [core_cut(both[:, n * size : (n + 1) * size], 1, mate) for n in range(len(weights))]
+            parts = [jnp.pad(p, ((0, 0), (0, pitch - p.shape[1]))) for p in parts]
+            return jnp.concatenate(parts, axis=1)
+
+        return jnp.concatenate([cut(False), exchange(cut(True), 1)], axis=0)
+
+    def row_weight(weight, far, filler):
+        both = jnp.concatenate([chip_cut(weight, 0, False), fill(far, filler)], axis=1)
+        return jnp.concatenate([core_cut(both, 0, False), exchange(core_cut(both, 0, True), 1)], axis=1)
+
+    joint_weight = column_weight([input_weight, branch_weight], joint_far, joint_fill, pitch)
+    out_weight = row_weight(output_weight, out_far, out_fill)
 
     def normalize(values, gain_vec):
         values = values.astype(f32)
         scale_rows = lax.rsqrt(jnp.sum(values * values, axis=1, keepdims=True) / model + norm_eps)
         return (values * scale_rows * gain_vec).astype(bf16), scale_rows
 
-    normed_mix, scale_mix = normalize(raw, gains[0])
+    normed_mix, scale_mix = normalize(jnp.concatenate([raw_even, raw_odd], axis=1), gains[0])
     joint = dot(normed_mix, joint_weight)
 
     def channels(values):
@@ -504,22 +498,30 @@
         channels(bias_x)[None],
         coef,
     )
-    middle = my_half(own).astype(f32) + plane_scatter([dot(mixed, out_weight[:, c]) for c in cols])
-
-    middle_full = plane_gather(middle.astype(bf16))
+    middle = my_half(own).astype(f32) + plane_scatter(
+        dot(mixed, out_weight[:, :half]), dot(mixed, out_weight[:, half:])
+    )
+
+    feed_weight = column_weight([gate_weight, up_weight], after(feed_far, mixed), feed_fill, feed_part)
+    last_weight = row_weight(down_weight, after(last_far, mixed), last_fill)
+    valid_rows = (lax.broadcasted_iota(jnp.int32, (length, 1), 0) < lengths[0]).astype(f32)
+    cotangent = grad_out[0]
+    wide_cotangent = jnp.concatenate(widen(after(cotangent, mixed)), axis=1)
+    grad_low = (wide_cotangent.astype(f32) * valid_rows).astype(bf16)
+
+    middle_full, _ = plane_gather(middle.astype(bf16))
     normed_mlp, scale_mlp_full = normalize(middle_full, gains[1])
     feed = dot(normed_mlp, feed_weight)
     gate_value, up_value = feed[:, :feed_part], feed[:, feed_part:]
     grad_hidden = dot(grad_low, last_weight, 1, 1)
     gate_act, gate_slope = gelu_parts(gate_value)
     hidden = (gate_act * up_value).astype(bf16)
-    grad_feed = jnp.concatenate(
-        [(grad_hidden * up_value * gate_slope).astype(bf16), (grad_hidden * gate_act).astype(bf16)], axis=1
-    )
-    grad_down = send_home([dot(hidden, grad_low[:, c], 0, 0) for c in cols])
-    grad_gate = send_home([dot(normed_mlp[:, c], grad_feed[:, :feed_part], 0, 0) for c in cols])
-    grad_up = send_home([dot(normed_mlp[:, c], grad_feed[:, feed_part:], 0, 0) for c in cols])
-    grad_normed_mlp = plane_scatter([dot(grad_feed, feed_weight[c], 1, 1) for c in cols])
+    grad_gate = (grad_hidden * up_value * gate_slope).astype(bf16)
+    grad_up = (grad_hidden * gate_act).astype(bf16)
+    grad_feed = jnp.concatenate([grad_gate, grad_up], axis=1)
+    grad_normed_mlp = plane_scatter(
+        dot(grad_feed, feed_weight[:half], 1, 1), dot(grad_feed, feed_weight[half:], 1, 1)
+    )
 
     unit_mlp = middle * my_half(scale_mlp_full)
     grad_top = my_half(cotangent).astype(f32) * my_half(valid_rows)
@@ -528,15 +530,14 @@
     grad_middle = grad_top + my_half(scale_mlp_full) * (scaled - unit_mlp * project[:, None])
     gain_mlp_part = jnp.sum(grad_normed_mlp * unit_mlp, axis=0)
 
-    grad_mid_full = plane_gather(grad_middle.astype(bf16))
+    grad_mid_full, gathered = plane_gather(grad_middle.astype(bf16))
     grad_mixed = dot(grad_mid_full, out_weight, 1, 1)
-    grad_output = send_home([dot(mixed, grad_mid_full[:, c], 0, 0) for c in cols])
     grad_joint, gate_low, input_low, small = mixer_backward(
         grad_mixed, joint, conv_low, sig_a, sig_x, decay, root, state, taps, gate_a_part, gate_x_part, coef, slope
     )
-    grad_normed_mix = plane_scatter([dot(grad_joint, joint_weight[c], 1, 1) for c in cols])
-    grad_joint_weight = send_home([dot(normed_mix[:, c], grad_joint, 0, 0) for c in cols])
-
+    grad_normed_mix = plane_scatter(
+        dot(grad_joint, joint_weight[:half], 1, 1), dot(grad_joint, joint_weight[half:], 1, 1)
+    )
     residual = my_half(own).astype(f32)
     scale_half = my_half(scale_mix)
     unit_mix = residual * scale_half
@@ -545,7 +546,56 @@
     grad_x = grad_middle + scale_half * (scaled - unit_mix * project[:, None])
     gain_mix_part = jnp.sum(grad_normed_mix * unit_mix, axis=0)
 
-    final = middle + plane_scatter([dot(hidden, last_weight[:, c]) for c in cols])
+    def pieces(left, right, axis):
+        both = []
+        for side in range(2):
+            part = []
+            for n in range(2):
+                cols = slice((2 * side + n) * wide, (2 * side + n + 1) * wide)
+                part.append(
+                    dot(left[:, cols], right, 0, 0) if axis == 0 else dot(left, right[:, cols], 0, 0)
+                )
+            both.append(jnp.stack(part).astype(bf16))
+        return both
+
+    def home(left, right, axis, *earlier):
+        even, odd = pieces(left, right, axis)
+        mate = exchange(odd, 1)
+        near = jnp.stack([even[0], mate[0]])
+        far = exchange(after(jnp.stack([even[1], mate[1]]), *earlier), 2)
+        return near, far
+
+    down_near, down_far = home(hidden, grad_low, 1, gathered)
+    gate_near, gate_far = home(normed_mlp, grad_gate, 0, gathered, down_far)
+    up_near, up_far = home(normed_mlp, grad_up, 0, gathered, gate_far)
+    out_near, out_far = home(mixed, grad_mid_full, 1)
+    joint_near, joint_far = home(normed_mix, grad_joint, 0)
+    chunks = [
+        down_near, gate_near, up_near, down_far, gate_far, up_far, out_near, out_far, joint_near, joint_far,
+    ]
+    sums, starts = [], []
+    for n, chunk in enumerate(chunks):
+        total, first = line_sum(after(chunk, starts[n - 2]) if n >= 2 else chunk)
+        sums.append(total)
+        starts.append(first)
+
+    def owned(near, far, axis):
+        near, far = near.astype(f32), far.astype(f32)
+        return in_order(near[0], near[1], far[0], far[1], axis)
+
+    grad_w_d = owned(sums[0], sums[3], 0)
+    grad_w_g = owned(sums[1], sums[4], 1)
+    grad_w_u = owned(sums[2], sums[5], 1)
+    grad_w_out = owned(sums[6], sums[7], 0)
+
+    def joint_columns(start):
+        cols = slice(start, start + mix_part)
+        return owned(sums[8][:, :, cols], sums[9][:, :, cols], 1)
+
+    late_hidden = after(hidden, gathered)
+    final = middle + plane_scatter(
+        dot(late_hidden, last_weight[:, :half]), dot(late_hidden, last_weight[:, half:])
+    )
     output = final.astype(bf16)
     output = halves(output, exchange(output, 0, across=True))[None]
     grad_inputs = grad_x.astype(bf16)
@@ -557,33 +607,34 @@
         for n in range(block_part):
             span = slice(n * block_size, (n + 1) * block_size)
             gate_blocks.append(dense[span, span])
-    gate_blocks = line_sum(jnp.stack(gate_blocks).astype(bf16))
-    gate_blocks = in_order([gate_blocks] + [exchange(gate_blocks, r) for r in range(1, groups)])
-    gate_blocks = jnp.stack(gate_blocks).astype(f32).reshape(groups, 2, block_part, block_size, block_size)
-    grad_gate_a = gate_blocks[:, 0].reshape(gate_a.shape)
-    grad_gate_x = gate_blocks[:, 1].reshape(gate_x.shape)
+    gate_blocks, _ = line_sum(jnp.stack(gate_blocks).astype(bf16))
+    gate_pair = jnp.stack([gate_blocks, exchange(gate_blocks, 1)])
+    gate_far = exchange(gate_pair, 2)
+    gate_all = in_order(gate_pair[:1], gate_pair[1:], gate_far[:1], gate_far[1:], 0).astype(f32)
+    gate_all = gate_all.reshape(groups, 2, block_part, block_size, block_size)
+    grad_gate_a = gate_all[:, 0].reshape(gate_a.shape)
+    grad_gate_x = gate_all[:, 1].reshape(gate_x.shape)
+
     half_valid = my_half(valid_rows)
-    first = jnp.logical_and(column == 0, lax.axis_index("gy") == 0)
-    stat_sums = jnp.stack(
-        [
-            jnp.sum(half_valid * final * final),
-            jnp.sum(half_valid * grad_x * grad_x),
-            jnp.where(first, jnp.sum(lengths).astype(f32), 0.0),
-        ]
-    )
-    small = lax.psum(place_part(small, (small.shape[0], conv_w.shape[1]), channel_start, 1), ("dp", "gx"))
-    grad_gains = lax.psum(jnp.stack([gain_mix_part, gain_mlp_part]), ("dp", "gy"))
-    totals = lax.psum(stat_sums, ("dp", "gx", "gy"))
-    token_count = totals[2] * model
+    tokens = jnp.where(lax.axis_index("gy") == 0, lengths[0].astype(f32), 0.0)
+    stats = [jnp.sum(half_valid * final * final), jnp.sum(half_valid * grad_x * grad_x), tokens]
+    shared = jnp.stack([gain_mix_part, gain_mlp_part] + [jnp.full((wide,), v, f32) for v in stats])
+    shared = shared + exchange(shared, 0, across=True)
+    small_rows = small.shape[0]
+    packed = jnp.concatenate([jnp.pad(small, ((0, 0), (0, wide - mix_part))), shared], axis=0)
+    packed, _ = line_sum(packed)
+    packed_pair = jnp.stack([packed, exchange(packed, 1)])
+    packed_far = exchange(packed_pair, 2)
+    totals = (packed_pair[0, :, 0] + packed_pair[1, :, 0]) + (packed_far[0, :, 0] + packed_far[1, :, 0])
+    small_pair, small_far = packed_pair[:, :small_rows, :mix_part], packed_far[:, :small_rows, :mix_part]
+    small = in_order(small_pair[0], small_pair[1], small_far[0], small_far[1], 1)
+    token_count = (totals[small_rows + 4] / groups) * model
     taps_count = conv_w.shape[0]
-
-    def joint_columns(start):
-        return jnp.concatenate([p[:, start : start + mix_part] for p in grad_joint_weight], axis=1)
 
     return (
         output,
         grad_inputs,
-        grad_gains[0],
+        packed[small_rows],
         joint_columns(0),
         joint_columns(pitch),
         small[:taps_count],
@@ -593,13 +644,13 @@
         grad_gate_x,
         small[taps_count + 2],
         small[taps_count + 3],
-        jnp.concatenate(grad_output, axis=0),
-        grad_gains[1],
-        jnp.concatenate(grad_gate, axis=1),
-        jnp.concatenate(grad_up, axis=1),
-        jnp.concatenate(grad_down, axis=0),
-        jnp.sqrt(totals[0] / token_count),
-        jnp.sqrt(totals[1] / token_count),
+        grad_w_out,
+        packed[small_rows + 1],
+        grad_w_g,
+        grad_w_u,
+        grad_w_d,
+        jnp.sqrt(totals[small_rows + 2] / token_count),
+        jnp.sqrt(totals[small_rows + 3] / token_count),
     )
 
 

time: 1480 us -> 898 us (0.61); the launches traced: 1460 us -> 893 us
  starting transfers between devices: 385 us -> 131 us
  blocking collectives: 174 us -> 0 us
  waiting for transfers between devices: 554 us -> 450 us
  local copies, waits for them, and re-layouts: 146 us -> 60.6 us
  other arithmetic: 80.4 us -> 136 us
    psum x3 -> x0, blocking collectives: 174 us -> none  [the longest x1 72.9 us: body(): lax.psum(jnp.stack([gain_mix_part, gain_mlp_part]), ('dp', 'gy'))]
    ppermute x21 -> x12, starting transfers between devices: 168 us -> 52.7 us  [line_sum(): lax.ppermute(value, 'dp', [(s, s + 1), (count - 1 - s, count - 2 - s)])]
    ppermute x36 -> x4, starting transfers between devices: 98 us -> 3.74 us  [from_neighbour(): lax.ppermute(value, 'dp', pairs)]
    dynamic_update_slice x60 -> x0, local copies, waits for them, and re-layouts: 86.1 us -> none  [the longest x39 71 us: put_rows(): lax.dynamic_update_slice(held, value, (r * wide + row, lane))]
    ppermute x6, waiting for transfers between devices: 75.4 us -> 28.1 us  [exchange(): lax.ppermute(value, ('gx', 'gy'), [(i * high + j, (i ^ flip) * high + (j...]
    ppermute x36 -> x4, waiting for transfers between devices: 64.7 us -> 24.9 us  [from_neighbour(): lax.ppermute(value, 'dp', pairs)]
    ppermute x21 -> x12, waiting for transfers between devices: 154 us -> 117 us  [line_sum(): lax.ppermute(value, 'dp', [(s, s + 1), (count - 1 - s, count - 2 - s)])]
    select_n x39 -> x33, other arithmetic: 26.1 us -> 59.7 us  [joined(): jnp.where(mine_first, jnp.concatenate([mine, other], axis=axis), jnp.conc...]
  transfers between devices with their start and end apart: 186 -> 101, of which waited for: 71 -> 39; matrix products, arithmetic and copies ran while one was open for 17% -> 26% of each run, Pallas kernels for 2% -> 4%
where the time goes in v2:
time: 898 us; the launch traced here: 893 us
  waiting for transfers between devices  450 us (50%)
  other arithmetic  136 us (15%)
  starting transfers between devices  131 us (15%)
  matrix products  73.9 us (8%)
  local copies, waits for them, and re-layouts  60.6 us (7%)
  Pallas kernels  33.5 us (4%)
    ppermute x12, waiting for transfers between devices, line_sum(): lax.ppermute(value, 'dp', [(half - 1 - s, half - 2 - s), (half + s, half...  147 us
    ppermute x12, waiting for transfers between devices, line_sum(): lax.ppermute(value, 'dp', [(s, s + 1), (count - 1 - s, count - 2 - s)])  117 us
    ppermute x44, waiting for transfers between devices, exchange(): return lax.ppermute(value, 'gx', [(i, i ^ flip) for i in range(wide)])  107 us
    dot_general x34, matrix products, dot(): lax.dot_general(left, right, (((left_dim,), (right_dim,)), ((), ())), pre...  73.9 us
    select_n x33, other arithmetic, joined(): jnp.where(mine_first, jnp.concatenate([mine, other], axis=axis), jnp.conc...  59.7 us
    ppermute x12, starting transfers between devices, line_sum(): lax.ppermute(value, 'dp', [(s, s + 1), (count - 1 - s, count - 2 - s)])  52.7 us
    ppermute x6, waiting for transfers between devices, exchange(): lax.ppermute(value, ('gx', 'gy'), [(i * high + j, (i ^ flip) * high + (j...  28.1 us
    ppermute x44, starting transfers between devices, exchange(): return lax.ppermute(value, 'gx', [(i, i ^ flip) for i in range(wide)])  27.8 us
  transfers between devices with their start and end apart: 101, of which 39 were waited for; matrix products, arithmetic and copies ran while one was open for 26% of the time, Pallas kernels for 4%

profile of v2, /device:TPU:0, one launch (start us, length us, event | category | flops | bytes accessed | tf_op | source)
XLA Modules:
  0.0 893.1 jit_solution(4617500426922435307)
XLA Ops:
  29.6 7.4 collective-permute-done.5
  73.0 15.3 %mixer_forward.1 = (bf16[1024,352]{1,0:T(8,128)(2,1)S(1)}, bf16[1024,352]{1,0:T(8,128)(2,1)S(1)}, f32[1024,352]{1,0:T(8,128)S(1)}, f32[1024,352]{1,0:T(8,128)S(1...) custom-call(f32[1024,768]{1,0:T(8,128)} %fusion.26.joint_ref, ...), custom_call_target="tpu_custom_call" | custom-call | flops 507510784 | bytes 11534336 | tf_op jit(solution)/shard_map/mixer_forward/pallas_call | solution.py:141
  92.5 11.0 %collective-permute-done.22 = bf16[512,512]{1,0:T(8,128)(2,1)} collective-permute-done((bf16[512,512]{1,0:T(8,128)(2,1)S(1)}, bf16[512,512]{1,0:T(8,128)(2,1)}, u32[]{:S(2)}, u32[]{:S(2)}) %collective-permute-start.22) | collective-permute-done | bytes 524320 | tf_op jit(solution)/shard_map/ppermute | solution.py:280
  108.7 8.3 collective-permute-done.23
  128.8 12.0 %pad_maximum_fusion = bf16[1024,3072]{1,0:T(8,128)(2,1)S(1)} fusion(bf16[512,3072]{1,0:T(8,128)(2,1)S(1)} %maximum_select_fusion.3, bf16[512,1536]{1,0:T(8,128)(2,1)S(1)} %get-tuple-element.181, bf16[512,1536]{1,0:T(8,128)(2,1)S(1)} %get-tuple-element.182), kind=kLoop, calls=%fused_computation.11 | loop fusion | flops 18874368 | bytes 12582912 | tf_op jit(solution)/shard_map/concatenate | solution.py:451
  148.4 11.6 %collective-permute-done.14 = bf16[512,512]{1,0:T(8,128)(2,1)S(1)} collective-permute-done((bf16[512,512]{1,0:T(8,128)(2,1)S(1)}, bf16[512,512]{1,0:T(8,128)(2,1)S(1)}, u32[]{:S(2)}, u32[]{:S(2)}) %collective-permute-start.14) | collective-permute-done | bytes 524320 | tf_op jit(solution)/shard_map/ppermute | solution.py:283
  160.0 10.0 %collective-permute-done.13 = bf16[512,512]{1,0:T(8,128)(2,1)S(1)} collective-permute-done((bf16[512,512]{1,0:T(8,128)(2,1)S(1)}, bf16[512,512]{1,0:T(8,128)(2,1)S(1)}, u32[]{:S(2)}, u32[]{:S(2)}) %collective-permute-start.13) | collective-permute-done | bytes 524320 | tf_op jit(solution)/shard_map/ppermute | solution.py:280
  179.5 16.9 %collective-permute-done.16 = bf16[512,512]{1,0:T(8,128)(2,1)S(1)} collective-permute-done((bf16[512,512]{1,0:T(8,128)(2,1)S(1)}, bf16[512,512]{1,0:T(8,128)(2,1)S(1)}, u32[]{:S(2)}, u32[]{:S(2)}) %collective-permute-start.16) | collective-permute-done | bytes 524320 | tf_op jit(solution)/shard_map/ppermute | solution.py:282
  198.9 9.5 %maximum_select_fusion.13 = bf16[1024,1024]{1,0:T(8,128)(2,1)} fusion(bf16[512,1024]{1,0:T(8,128)(2,1)S(1)} %constant_dynamic-update-slice_fusion, bf16[512,512]{1,0:T(8,128)(2,1)S(1)} %collective-permute-done.15, bf16[512,512]{1,0:T(8,128)(2,1)S(1)} %get-tuple-element.87, pred[]{:T(512)S(6)} %eq.43), kind=kLoop, calls=%fused_computation.104 | loop fusion | flops 13631488 | bytes 4194305 | tf_op jit(solution)/shard_map/jit(_where)/select_n | solution.py:317
  211.2 17.5 %collective-permute-done.26 = bf16[768,512]{1,0:T(8,128)(2,1)} collective-permute-done((bf16[768,512]{1,0:T(8,128)(2,1)}, bf16[768,512]{1,0:T(8,128)(2,1)}, u32[]{:S(2)}, u32[]{:S(2)}) %collective-permute-start.26) | collective-permute-done | bytes 786464 | tf_op jit(solution)/shard_map/ppermute | solution.py:371
  240.8 8.5 fusion.6
  289.6 8.8 collective-permute-done.31
  301.2 8.1 collective-permute-done.30
  316.0 8.0 collective-permute-done.71
  327.6 28.7 %collective-permute-done.61 = bf16[2,768,512]{2,1,0:T(8,128)(2,1)S(1)} collective-permute-done((bf16[2,768,512]{2,1,0:T(8,128)(2,1)S(1)}, bf16[2,768,512]{2,1,0:T(8,128)(2,1)S(1)}, u32[]{:S(2)}, u32[]{:S(2)}) %collective-permute-start.61) | collective-permute-done | bytes 1572896 | tf_op jit(solution)/shard_map/ppermute | solution.py:303
  365.6 8.3 maximum_select_fusion.14
  380.1 13.2 %collective-permute-done.62 = bf16[2,512,768]{2,1,0:T(8,128)(2,1)S(1)} collective-permute-done((bf16[2,512,768]{2,1,0:T(8,128)(2,1)S(1)}, bf16[2,512,768]{2,1,0:T(8,128)(2,1)S(1)}, u32[]{:S(2)}, u32[]{:S(2)}) %collective-permute-start.62) | collective-permute-done | bytes 1572896 | tf_op jit(solution)/shard_map/ppermute | solution.py:303
  398.8 12.0 %collective-permute-done.58 = bf16[2,768,512]{2,1,0:T(8,128)(2,1)S(1)} collective-permute-done((bf16[2,768,512]{2,1,0:T(8,128)(2,1)S(1)}, bf16[2,768,512]{2,1,0:T(8,128)(2,1)S(1)}, u32[]{:S(2)}, u32[]{:S(2)}) %collective-permute-start.58) | collective-permute-done | bytes 1572896 | tf_op jit(solution)/shard_map/ppermute | solution.py:280
  421.0 18.2 %mixer_backward.1 = (bf16[1024,768]{1,0:T(8,128)(2,1)}, bf16[1024,352]{1,0:T(8,128)(2,1)}, bf16[1024,352]{1,0:T(8,128)(2,1)}, f32[8,352]{1,0:T(8,128)}) custom-call(f32[1024,352]{1,0:T(8,128)} %fusion.12.grad_mixed_ref, f32[1024,768]{1,0:T(8,128)} %fusion.26.joint_ref, bf16[1024,352]{1,0:T(8,128)(2,1)} %copy-done.6, f32[1024,352]{1,0:T(8,128)} %copy-done.2, ...), custom_call_target="tpu_custom_call" | custom-call | flops 507510784 | bytes 14417920 | tf_op jit(solution)/shard_map/mixer_backward/pallas_call | solution.py:258
  468.3 19.0 %collective-permute-done.82 = bf16[4,176,176]{2,1,0:T(8,128)(2,1)S(1)} collective-permute-done((bf16[4,176,176]{2,1,0:T(8,128)(2,1)S(1)}, bf16[4,176,176]{2,1,0:T(8,128)(2,1)S(1)}, u32[]{:S(2)}, u32[]{:S(2)}) %collective-permute-start.82) | collective-permute-done | bytes 247840 | tf_op jit(solution)/shard_map/ppermute | solution.py:310
  505.6 19.6 %collective-permute-done.72 = bf16[2,768,512]{2,1,0:T(8,128)(2,1)} collective-permute-done((bf16[2,768,512]{2,1,0:T(8,128)(2,1)S(1)}, bf16[2,768,512]{2,1,0:T(8,128)(2,1)}, u32[]{:S(2)}, u32[]{:S(2)}) %collective-permute-start.72) | collective-permute-done | bytes 1572896 | tf_op jit(solution)/shard_map/ppermute | solution.py:303
  538.7 7.6 collective-permute-done.46
  547.9 9.8 %collective-permute-done.45 = bf16[512,512]{1,0:T(8,128)(2,1)S(1)} collective-permute-done((bf16[512,512]{1,0:T(8,128)(2,1)S(1)}, bf16[512,512]{1,0:T(8,128)(2,1)S(1)}, u32[]{:S(2)}, u32[]{:S(2)}) %collective-permute-start.45) | collective-permute-done | bytes 524320 | tf_op jit(solution)/shard_map/ppermute | solution.py:280
  563.5 16.7 %collective-permute-done.48 = f32[512]{0:T(512)S(1)} collective-permute-done((f32[512]{0:T(512)S(1)}, f32[512]{0:T(512)S(1)}, u32[]{:S(2)}, u32[]{:S(2)}) %collective-permute-start.48) | collective-permute-done | bytes 2080 | tf_op jit(solution)/shard_map/ppermute | solution.py:280
  599.6 13.4 %collective-permute-done.70 = bf16[2,512,768]{2,1,0:T(8,128)(2,1)} collective-permute-done((bf16[2,512,768]{2,1,0:T(8,128)(2,1)}, bf16[2,512,768]{2,1,0:T(8,128)(2,1)}, u32[]{:S(2)}, u32[]{:S(2)}) %collective-permute-start.70) | collective-permute-done | bytes 1572896 | tf_op jit(solution)/shard_map/ppermute | solution.py:280
  638.7 27.7 %collective-permute-done.64 = bf16[2,352,512]{2,1,0:T(8,128)(2,1)S(1)} collective-permute-done((bf16[2,352,512]{2,1,0:T(8,128)(2,1)S(1)}, bf16[2,352,512]{2,1,0:T(8,128)(2,1)S(1)}, u32[]{:S(2)}, u32[]{:S(2)}) %collective-permute-start.64) | collective-permute-done | bytes 720928 | tf_op jit(solution)/shard_map/ppermute | solution.py:303
  677.7 10.2 %collective-permute-done.69 = bf16[2,352,512]{2,1,0:T(8,128)(2,1)S(1)} collective-permute-done((bf16[2,352,512]{2,1,0:T(8,128)(2,1)S(1)}, bf16[2,352,512]{2,1,0:T(8,128)(2,1)S(1)}, u32[]{:S(2)}, u32[]{:S(2)}) %collective-permute-start.69) | collective-permute-done | bytes 720928 | tf_op jit(solution)/shard_map/ppermute | solution.py:280
  722.0 17.3 %collective-permute-done.74 = bf16[2,352,512]{2,1,0:T(8,128)(2,1)S(1)} collective-permute-done((bf16[2,352,512]{2,1,0:T(8,128)(2,1)S(1)}, bf16[2,352,512]{2,1,0:T(8,128)(2,1)S(1)}, u32[]{:S(2)}, u32[]{:S(2)}) %collective-permute-start.74) | collective-permute-done | bytes 720928 | tf_op jit(solution)/shard_map/ppermute | solution.py:303
  759.7 34.1 %collective-permute-done.88 = bf16[2,352,512]{2,1,0:T(8,128)(2,1)S(1)} collective-permute-done((bf16[2,352,512]{2,1,0:T(8,128)(2,1)S(1)}, bf16[2,352,512]{2,1,0:T(8,128)(2,1)S(1)}, u32[]{:S(2)}, u32[]{:S(2)}) %collective-permute-start.88) | collective-permute-done | bytes 720928 | tf_op jit(solution)/shard_map/ppermute | solution.py:310
  799.1 28.4 %collective-permute-done.96 = bf16[2,512,768]{2,1,0:T(8,128)(2,1)S(1)} collective-permute-done((bf16[2,512,768]{2,1,0:T(8,128)(2,1)S(1)}, bf16[2,512,768]{2,1,0:T(8,128)(2,1)S(1)}, u32[]{:S(2)}, u32[]{:S(2)}) %collective-permute-start.96) | collective-permute-done | bytes 1572896 | tf_op jit(solution)/shard_map/ppermute | solution.py:310
  833.3 27.9 %collective-permute-done.67 = bf16[2,512,768]{2,1,0:T(8,128)(2,1)S(1)} collective-permute-done((bf16[2,512,768]{2,1,0:T(8,128)(2,1)S(1)}, bf16[2,512,768]{2,1,0:T(8,128)(2,1)S(1)}, u32[]{:S(2)}, u32[]{:S(2)}) %collective-permute-start.67) | collective-permute-done | bytes 1572896 | tf_op jit(solution)/shard_map/ppermute | solution.py:310
  863.1 20.4 %collective-permute-done.77 = bf16[2,512,768]{2,1,0:T(8,128)(2,1)S(1)} collective-permute-done((bf16[2,512,768]{2,1,0:T(8,128)(2,1)S(1)}, bf16[2,512,768]{2,1,0:T(8,128)(2,1)S(1)}, u32[]{:S(2)}, u32[]{:S(2)}) %collective-permute-start.77) | collective-permute-done | bytes 1572896 | tf_op jit(solution)/shard_map/ppermute | solution.py:310
  (577 shorter events, 399.2 us)
Async XLA Ops:
  18.3 70.0 %collective-permute-start.19 = (bf16[256,3072]{1,0:T(8,128)(2,1)}, bf16[256,3072]{1,0:T(8,128)(2,1)}, u32[]{:S(2)}, u32[]{:S(2)}) collective-permute-start(bf16[256,3072]{1,0:T(8,128)(2,1)} %pad_maximum_fusion.12), channel_id=1, source_target_pairs={{0,4},{2,6},{4,0},{6,2},{1,5},{3,7},{5,1},{7,3},{8,12},{10,14},{12... | collective-permute-start | bytes 4718600 | tf_op jit(solution)/shard_map/ppermute | solution.py:280
  92.4 48.4 %collective-permute-start.11 = (bf16[1024,1024]{1,0:T(8,128)(2,1)}, bf16[1024,1024]{1,0:T(8,128)(2,1)}, u32[]{:S(2)}, u32[]{:S(2)}) collective-permute-start(bf16[1024,1024]{1,0:T(8,128)(2,1)} %convolution_convert_fusion), channel_id=1, source_target_pairs={{0,2},{2,0},{4,6},{6,4},{1,3},{3,1},{5,7},{7,5},{8,10},{10,8},{12,... | collective-permute-start | bytes 6291464 | tf_op jit(solution)/shard_map/ppermute | solution.py:280
  106.0 102.4 %collective-permute-start.25 = (bf16[768,512]{1,0:T(8,128)(2,1)}, bf16[768,512]{1,0:T(8,128)(2,1)}, u32[]{:S(2)}, u32[]{:S(2)}) collective-permute-start(bf16[768,512]{1,0:T(8,128)(2,1)} %constant_dynamic-slice_fusion.6), channel_id=1, source_target_pairs={{0,4},{2,6},{4,0},{6,2},{1,5},{3,7},{5,1},{7,3},{8,12},{10,14},{12... | collective-permute-start | bytes 2359304 | tf_op jit(solution)/shard_map/ppermute | solution.py:280
  120.6 110.9 %collective-permute-start.24 = (bf16[1024,1024]{1,0:T(8,128)(2,1)}, bf16[1024,1024]{1,0:T(8,128)(2,1)}, u32[]{:S(2)}, u32[]{:S(2)}) collective-permute-start(bf16[1024,1024]{1,0:T(8,128)(2,1)} %pad_maximum_fusion.7), channel_id=1, source_target_pairs={{0,2},{2,0},{4,6},{6,4},{1,3},{3,1},{5,7},{7,5},{8,10},{10,8},{12,... | collective-permute-start | bytes 6291464 | tf_op jit(solution)/shard_map/ppermute | solution.py:280
  196.3 44.4 %collective-permute-start.21 = (bf16[1024,1536]{1,0:T(8,128)(2,1)}, bf16[1024,1536]{1,0:T(8,128)(2,1)}, u32[]{:S(2)}, u32[]{:S(2)}) collective-permute-start(bf16[1024,1536]{1,0:T(8,128)(2,1)} %pad_maximum_fusion.3), channel_id=1, source_target_pairs={{0,2},{2,0},{4,6},{6,4},{1,3},{3,1},{5,7},{7,5},{8,10},{10,8},{12,... | collective-permute-start | bytes 9437192 | tf_op jit(solution)/shard_map/ppermute | solution.py:280
  298.4 58.0 %collective-permute-start.61 = (bf16[2,768,512]{2,1,0:T(8,128)(2,1)S(1)}, bf16[2,768,512]{2,1,0:T(8,128)(2,1)S(1)}, u32[]{:S(2)}, u32[]{:S(2)}) collective-permute-start(bf16[2,768,512]{2,1,0:T(8,128)(2,1)S(1)} %pad_maximum_fusion.21), channel_id=1, source_target_pairs={{0,8},{24,16},{1,9},{25,17},{2,10},{26,18},{3,11},{27,19},{4,12},{... | collective-permute-start | bytes 4718600 | tf_op jit(solution)/shard_map/ppermute | solution.py:303
  315.5 46.0 %collective-permute-start.34 = (bf16[512,512]{1,0:T(8,128)(2,1)S(1)}, bf16[512,512]{1,0:T(8,128)(2,1)S(1)}, u32[]{:S(2)}, u32[]{:S(2)}) collective-permute-start(bf16[512,512]{1,0:T(8,128)(2,1)S(1)} %get-tuple-element.84), channel_id=1, source_target_pairs={{0,4},{2,6},{4,0},{6,2},{1,5},{3,7},{5,1},{7,3},{8,12},{10,14},{12... | collective-permute-start | bytes 1572872 | tf_op jit(solution)/shard_map/ppermute | solution.py:280
  324.4 50.0 %collective-permute-start.89 = (bf16[2,512,768]{2,1,0:T(8,128)(2,1)S(1)}, bf16[2,512,768]{2,1,0:T(8,128)(2,1)S(1)}, u32[]{:S(2)}, u32[]{:S(2)}) collective-permute-start(bf16[2,512,768]{2,1,0:T(8,128)(2,1)S(1)} %add_convert_fusion.11), channel_id=1, source_target_pairs={{8,16},{16,8},{9,17},{17,9},{10,18},{18,10},{11,19},{19,11},{12,20... | collective-permute-start | bytes 4718600 | tf_op jit(solution)/shard_map/ppermute | solution.py:306
  325.5 39.9 %collective-permute-start.40 = (bf16[512,512]{1,0:T(8,128)(2,1)S(1)}, bf16[512,512]{1,0:T(8,128)(2,1)S(1)}, u32[]{:S(2)}, u32[]{:S(2)}) collective-permute-start(bf16[512,512]{1,0:T(8,128)(2,1)S(1)} %get-tuple-element.84), channel_id=1, source_target_pairs={{0,1},{1,0},{2,3},{3,2},{4,5},{5,4},{6,7},{7,6},{8,9},{9,8},{10,11... | collective-permute-start | bytes 1572872 | tf_op jit(solution)/shard_map/ppermute | solution.py:282
  365.4 47.1 %collective-permute-start.35 = (bf16[1024,1024]{1,0:T(8,128)(2,1)}, bf16[1024,1024]{1,0:T(8,128)(2,1)}, u32[]{:S(2)}, u32[]{:S(2)}) collective-permute-start(bf16[1024,1024]{1,0:T(8,128)(2,1)} %convolution_convert_fusion.2), channel_id=1, source_target_pairs={{0,2},{2,0},{4,6},{6,4},{1,3},{3,1},{5,7},{7,5},{8,10},{10,8},{12,... | collective-permute-start | bytes 6291464 | tf_op jit(solution)/shard_map/ppermute | solution.py:280
  373.9 42.5 %collective-permute-start.42 = (bf16[1024,1024]{1,0:T(8,128)(2,1)S(1)}, bf16[1024,1024]{1,0:T(8,128)(2,1)S(1)}, u32[]{:S(2)}, u32[]{:S(2)}) collective-permute-start(bf16[1024,1024]{1,0:T(8,128)(2,1)S(1)} %maximum_select_fusion.14), channel_id=1, source_target_pairs={{0,2},{2,0},{4,6},{6,4},{1,3},{3,1},{5,7},{7,5},{8,10},{10,8},{12,... | collective-permute-start | bytes 6291464 | tf_op jit(solution)/shard_map/ppermute | solution.py:280
  393.3 99.0 %collective-permute-start.90 = (bf16[2,512,768]{2,1,0:T(8,128)(2,1)}, bf16[2,512,768]{2,1,0:T(8,128)(2,1)}, u32[]{:S(2)}, u32[]{:S(2)}) collective-permute-start(bf16[2,512,768]{2,1,0:T(8,128)(2,1)} %add_convert_fusion.10), channel_id=1, source_target_pairs={{8,0},{16,24},{9,1},{17,25},{10,2},{18,26},{11,3},{19,27},{12,4},{... | collective-permute-start | bytes 4718600 | tf_op jit(solution)/shard_map/ppermute | solution.py:310
  395.0 103.8 %collective-permute-start.93 = (bf16[2,512,768]{2,1,0:T(8,128)(2,1)S(1)}, bf16[2,512,768]{2,1,0:T(8,128)(2,1)}, u32[]{:S(2)}, u32[]{:S(2)}) collective-permute-start(bf16[2,512,768]{2,1,0:T(8,128)(2,1)S(1)} %add_convert_fusion.7), channel_id=1, source_target_pairs={{8,16},{16,8},{9,17},{17,9},{10,18},{18,10},{11,19},{19,11},{12,20... | collective-permute-start | bytes 4718600 | tf_op jit(solution)/shard_map/ppermute | solution.py:306
  410.9 83.5 %collective-permute-start.98 = (bf16[2,768,512]{2,1,0:T(8,128)(2,1)}, bf16[2,768,512]{2,1,0:T(8,128)(2,1)}, u32[]{:S(2)}, u32[]{:S(2)}) collective-permute-start(bf16[2,768,512]{2,1,0:T(8,128)(2,1)} %add_convert_fusion.2), channel_id=1, source_target_pairs={{8,0},{16,24},{9,1},{17,25},{10,2},{18,26},{11,3},{19,27},{12,4},{... | collective-permute-start | bytes 4718600 | tf_op jit(solution)/shard_map/ppermute | solution.py:310
  494.3 41.7 %collective-permute-start.54 = (bf16[2,512,768]{2,1,0:T(8,128)(2,1)S(1)}, bf16[2,512,768]{2,1,0:T(8,128)(2,1)S(1)}, u32[]{:S(2)}, u32[]{:S(2)}) collective-permute-start(bf16[2,512,768]{2,1,0:T(8,128)(2,1)S(1)} %pad_maximum_fusion.13), channel_id=1, source_target_pairs={{0,2},{2,0},{4,6},{6,4},{1,3},{3,1},{5,7},{7,5},{8,10},{10,8},{12,... | collective-permute-start | bytes 4718600 | tf_op jit(solution)/shard_map/ppermute | solution.py:280
  504.3 58.7 %collective-permute-start.94 = (bf16[2,512,768]{2,1,0:T(8,128)(2,1)S(1)}, bf16[2,512,768]{2,1,0:T(8,128)(2,1)S(1)}, u32[]{:S(2)}, u32[]{:S(2)}) collective-permute-start(bf16[2,512,768]{2,1,0:T(8,128)(2,1)S(1)} %add_convert_fusion.6), channel_id=1, source_target_pairs={{8,0},{16,24},{9,1},{17,25},{10,2},{18,26},{11,3},{19,27},{12,4},{... | collective-permute-start | bytes 4718600 | tf_op jit(solution)/shard_map/ppermute | solution.py:310
  536.1 51.9 %collective-permute-start.38 = (bf16[512,512]{1,0:T(8,128)(2,1)S(1)}, bf16[512,512]{1,0:T(8,128)(2,1)S(1)}, u32[]{:S(2)}, u32[]{:S(2)}) collective-permute-start(bf16[512,512]{1,0:T(8,128)(2,1)S(1)} %copy-done.48), channel_id=1, source_target_pairs={{0,5},{1,4},{2,7},{3,6},{4,1},{5,0},{6,3},{7,2},{8,13},{9,12},{10,... | collective-permute-start | bytes 1572872 | tf_op jit(solution)/shard_map/ppermute | solution.py:283
  546.4 43.4 %collective-permute-start.37 = (bf16[512,512]{1,0:T(8,128)(2,1)S(1)}, bf16[512,512]{1,0:T(8,128)(2,1)S(1)}, u32[]{:S(2)}, u32[]{:S(2)}) collective-permute-start(bf16[512,512]{1,0:T(8,128)(2,1)S(1)} %copy-done.47), channel_id=1, source_target_pairs={{0,4},{2,6},{4,0},{6,2},{1,5},{3,7},{5,1},{7,3},{8,12},{10,14},{12... | collective-permute-start | bytes 1572872 | tf_op jit(solution)/shard_map/ppermute | solution.py:280
  563.0 49.9 %collective-permute-start.70 = (bf16[2,512,768]{2,1,0:T(8,128)(2,1)}, bf16[2,512,768]{2,1,0:T(8,128)(2,1)}, u32[]{:S(2)}, u32[]{:S(2)}) collective-permute-start(bf16[2,512,768]{2,1,0:T(8,128)(2,1)} %pad_maximum_fusion.23), channel_id=1, source_target_pairs={{0,4},{2,6},{4,0},{6,2},{1,5},{3,7},{5,1},{7,3},{8,12},{10,14},{12... | collective-permute-start | bytes 4718600 | tf_op jit(solution)/shard_map/ppermute | solution.py:280
  612.9 80.5 %collective-permute-start.73 = (bf16[2,512,768]{2,1,0:T(8,128)(2,1)}, bf16[2,512,768]{2,1,0:T(8,128)(2,1)S(1)}, u32[]{:S(2)}, u32[]{:S(2)}) collective-permute-start(bf16[2,512,768]{2,1,0:T(8,128)(2,1)} %collective-permute-done.70), channel_id=1, source_target_pairs={{0,8},{24,16},{1,9},{25,17},{2,10},{26,18},{3,11},{27,19},{4,12},{... | collective-permute-start | bytes 4718600 | tf_op jit(solution)/shard_map/ppermute | solution.py:303
  617.5 48.9 %collective-permute-start.64 = (bf16[2,352,512]{2,1,0:T(8,128)(2,1)S(1)}, bf16[2,352,512]{2,1,0:T(8,128)(2,1)S(1)}, u32[]{:S(2)}, u32[]{:S(2)}) collective-permute-start(bf16[2,352,512]{2,1,0:T(8,128)(2,1)S(1)} %copy-done.29), channel_id=1, source_target_pairs={{0,8},{24,16},{1,9},{25,17},{2,10},{26,18},{3,11},{27,19},{4,12},{... | collective-permute-start | bytes 2162696 | tf_op jit(solution)/shard_map/ppermute | solution.py:303
  624.6 70.2 %collective-permute-start.91 = (bf16[2,512,768]{2,1,0:T(8,128)(2,1)S(1)}, bf16[2,512,768]{2,1,0:T(8,128)(2,1)S(1)}, u32[]{:S(2)}, u32[]{:S(2)}) collective-permute-start(bf16[2,512,768]{2,1,0:T(8,128)(2,1)S(1)} %add_convert_fusion.9), channel_id=1, source_target_pairs={{8,16},{16,8},{9,17},{17,9},{10,18},{18,10},{11,19},{19,11},{12,20... | collective-permute-start | bytes 4718600 | tf_op jit(solution)/shard_map/ppermute | solution.py:306
  677.0 63.5 %collective-permute-start.68 = (bf16[2,512,768]{2,1,0:T(8,128)(2,1)S(1)}, bf16[2,512,768]{2,1,0:T(8,128)(2,1)S(1)}, u32[]{:S(2)}, u32[]{:S(2)}) collective-permute-start(bf16[2,512,768]{2,1,0:T(8,128)(2,1)S(1)} %copy-done.35), channel_id=1, source_target_pairs={{0,4},{2,6},{4,0},{6,2},{1,5},{3,7},{5,1},{7,3},{8,12},{10,14},{12... | collective-permute-start | bytes 4718600 | tf_op jit(solution)/shard_map/ppermute | solution.py:280
  687.8 59.9 %collective-permute-start.65 = (bf16[2,512,768]{2,1,0:T(8,128)(2,1)S(1)}, bf16[2,512,768]{2,1,0:T(8,128)(2,1)S(1)}, u32[]{:S(2)}, u32[]{:S(2)}) collective-permute-start(bf16[2,512,768]{2,1,0:T(8,128)(2,1)S(1)} %copy-done.24), channel_id=1, source_target_pairs={{0,8},{24,16},{1,9},{25,17},{2,10},{26,18},{3,11},{27,19},{4,12},{... | collective-permute-start | bytes 4718600 | tf_op jit(solution)/shard_map/ppermute | solution.py:303
  694.8 44.5 %collective-permute-start.74 = (bf16[2,352,512]{2,1,0:T(8,128)(2,1)S(1)}, bf16[2,352,512]{2,1,0:T(8,128)(2,1)S(1)}, u32[]{:S(2)}, u32[]{:S(2)}) collective-permute-start(bf16[2,352,512]{2,1,0:T(8,128)(2,1)S(1)} %collective-permute-done.69), channel_id=1, source_target_pairs={{0,8},{24,16},{1,9},{25,17},{2,10},{26,18},{3,11},{27,19},{4,12},{... | collective-permute-start | bytes 2162696 | tf_op jit(solution)/shard_map/ppermute | solution.py:303
  705.6 46.9 %collective-permute-start.92 = (bf16[2,512,768]{2,1,0:T(8,128)(2,1)S(1)}, bf16[2,512,768]{2,1,0:T(8,128)(2,1)S(1)}, u32[]{:S(2)}, u32[]{:S(2)}) collective-permute-start(bf16[2,512,768]{2,1,0:T(8,128)(2,1)S(1)} %add_convert_fusion.8), channel_id=1, source_target_pairs={{8,0},{16,24},{9,1},{17,25},{10,2},{18,26},{11,3},{19,27},{12,4},{... | collective-permute-start | bytes 4718600 | tf_op jit(solution)/shard_map/ppermute | solution.py:310
  740.5 53.7 %collective-permute-start.75 = (bf16[2,512,768]{2,1,0:T(8,128)(2,1)S(1)}, bf16[2,512,768]{2,1,0:T(8,128)(2,1)S(1)}, u32[]{:S(2)}, u32[]{:S(2)}) collective-permute-start(bf16[2,512,768]{2,1,0:T(8,128)(2,1)S(1)} %collective-permute-done.68), channel_id=1, source_target_pairs={{0,8},{24,16},{1,9},{25,17},{2,10},{26,18},{3,11},{27,19},{4,12},{... | collective-permute-start | bytes 4718600 | tf_op jit(solution)/shard_map/ppermute | solution.py:303
  748.1 49.3 %collective-permute-start.66 = (bf16[2,512,768]{2,1,0:T(8,128)(2,1)S(1)}, bf16[2,512,768]{2,1,0:T(8,128)(2,1)S(1)}, u32[]{:S(2)}, u32[]{:S(2)}) collective-permute-start(bf16[2,512,768]{2,1,0:T(8,128)(2,1)S(1)} %add_convert_fusion.15), channel_id=1, source_target_pairs={{8,16},{16,8},{9,17},{17,9},{10,18},{18,10},{11,19},{19,11},{12,20... | collective-permute-start | bytes 4718600 | tf_op jit(solution)/shard_map/ppermute | solution.py:306
  749.1 44.7 %collective-permute-start.88 = (bf16[2,352,512]{2,1,0:T(8,128)(2,1)S(1)}, bf16[2,352,512]{2,1,0:T(8,128)(2,1)S(1)}, u32[]{:S(2)}, u32[]{:S(2)}) collective-permute-start(bf16[2,352,512]{2,1,0:T(8,128)(2,1)S(1)} %add_convert_fusion.16), channel_id=1, source_target_pairs={{8,0},{16,24},{9,1},{17,25},{10,2},{18,26},{11,3},{19,27},{12,4},{... | collective-permute-start | bytes 2162696 | tf_op jit(solution)/shard_map/ppermute | solution.py:310
  753.4 74.1 %collective-permute-start.96 = (bf16[2,512,768]{2,1,0:T(8,128)(2,1)S(1)}, bf16[2,512,768]{2,1,0:T(8,128)(2,1)S(1)}, u32[]{:S(2)}, u32[]{:S(2)}) collective-permute-start(bf16[2,512,768]{2,1,0:T(8,128)(2,1)S(1)} %add_convert_fusion.4), channel_id=1, source_target_pairs={{8,0},{16,24},{9,1},{17,25},{10,2},{18,26},{11,3},{19,27},{12,4},{... | collective-permute-start | bytes 4718600 | tf_op jit(solution)/shard_map/ppermute | solution.py:310
  797.8 63.4 %collective-permute-start.67 = (bf16[2,512,768]{2,1,0:T(8,128)(2,1)S(1)}, bf16[2,512,768]{2,1,0:T(8,128)(2,1)S(1)}, u32[]{:S(2)}, u32[]{:S(2)}) collective-permute-start(bf16[2,512,768]{2,1,0:T(8,128)(2,1)S(1)} %add_convert_fusion.14), channel_id=1, source_target_pairs={{8,0},{16,24},{9,1},{17,25},{10,2},{18,26},{11,3},{19,27},{12,4},{... | collective-permute-start | bytes 4718600 | tf_op jit(solution)/shard_map/ppermute | solution.py:310
  828.8 54.6 %collective-permute-start.77 = (bf16[2,512,768]{2,1,0:T(8,128)(2,1)S(1)}, bf16[2,512,768]{2,1,0:T(8,128)(2,1)S(1)}, u32[]{:S(2)}, u32[]{:S(2)}) collective-permute-start(bf16[2,512,768]{2,1,0:T(8,128)(2,1)S(1)} %add_convert_fusion.12), channel_id=1, source_target_pairs={{8,0},{16,24},{9,1},{17,25},{10,2},{18,26},{11,3},{19,27},{12,4},{... | collective-permute-start | bytes 4718600 | tf_op jit(solution)/shard_map/ppermute | solution.py:310
  (147 other events, 2448.4 us)
